TPU v7x, 256 devices: a whole 4x4x8 slice. The times are simulated.
256 devices in a mesh: dp: 8 (over y, x_lo), fsdp: 32 (over z, x_hi, core).
Axes of the slice: x: 4 (x_hi: 2, x_lo: 2; x = x_hi * 2 + x_lo), y: 4, z: 8, core: 2. Of those that a mesh axis runs over, the one named last changes fastest.
Arguments:
- features: bfloat16 [32768, 640], P(('dp', 'fsdp')), may hold values from -6 to 6
- heights: int32 [256, 4], P(('dp', 'fsdp')), may hold values from 0 to 32, as said below
- widths: int32 [256, 4], P(('dp', 'fsdp')), may hold values from 0 to 32, as said below
- timesteps: int32 [256, 4], P(('dp', 'fsdp')), may hold values from 0 to 999
- norm_gain: float32 [640], replicated, may hold values from 0.1 to 1.9
- norm_shift: float32 [640], replicated, may hold values from -3 to 3
- conv_weight: bfloat16 [768, 5760], P('fsdp'), may hold values from -0.078125 to 0.078125
- time_weight: bfloat16 [768, 320], P('fsdp'), may hold values from -0.3125 to 0.3125
- cotangent: bfloat16 [32768, 768], P(('dp', 'fsdp')), may hold values from -6 to 6
Outputs:
- block_out: bfloat16 [32768, 768], P(('dp', 'fsdp'))
- grad_features: bfloat16 [32768, 640], P(('dp', 'fsdp'))
- grad_conv: float32 [768, 5760], P('fsdp')
- grad_time: float32 [768, 320], P('fsdp')
- grad_gain: float32 [640], replicated
- grad_shift: float32 [640], replicated
Inputs may be any that keep to these rules, and one draw needn't show every extreme that they name: In each block the live pixels heights * widths sum to at most 128, and in some block to exactly 128; every block has one or more images, slot after slot; an empty slot has height and width 0; sides are powers of two. `widths`: as for heights; a live image has width 2 or more.
All inputs are finite; a program needn't handle non-finite values.
Results may differ from a plain program's by a relative error of at most 0.0045.
Values may be sent and summed in bfloat16 or wider, within the bound.
A program may use at most 128 MiB of HBM per device.

v0:
```python
import math

import jax
import jax.numpy as jnp
from jax import lax
from jax.sharding import PartitionSpec as P

CO = 768
GROUPS = 32


highest = lax.Precision.HIGHEST


def layout(heights_row, widths_row, rows):
    images = heights_row.shape[0]
    area = heights_row * widths_row
    ends = jnp.cumsum(area)
    starts = ends - area
    position = jnp.arange(rows, dtype=jnp.int32)
    image = jnp.sum((position[:, None] >= ends[None, :]).astype(jnp.int32), axis=1)
    live = position < ends[images - 1]
    member = (image[:, None] == jnp.arange(images, dtype=jnp.int32)[None, :]) & live[:, None]
    first = jnp.sum(jnp.where(member, starts[None, :], 0), axis=1)
    height = jnp.sum(jnp.where(member, heights_row[None, :], 0), axis=1)
    width = jnp.sum(jnp.where(member, widths_row[None, :], 0), axis=1)
    offset = position - first
    width_safe = jnp.maximum(width, 1)
    row_index = offset // width_safe
    column = offset - row_index * width_safe
    targets = []
    for shift_row in (-1, 0, 1):
        for shift_col in (-1, 0, 1):
            near_row = row_index + shift_row
            near_col = column + shift_col
            valid = (
                live & (near_row >= 0) & (near_row < height) & (near_col >= 0) & (near_col < width)
            )
            targets.append(jnp.where(valid, first + near_row * width + near_col, rows))
    neighbours = jnp.stack(targets, axis=1)
    return (neighbours, live, member.astype(jnp.float32))


def timestep_features(times_row, feature_count):
    half = feature_count // 2
    rates = jnp.exp(-math.log(10000.0) * jnp.arange(half, dtype=jnp.float32) / half)
    angles = times_row.astype(jnp.float32)[:, None] * rates[None, :]
    return jnp.concatenate([jnp.sin(angles), jnp.cos(angles)], axis=1).astype(jnp.bfloat16)


def group_mean(values, member, counts):
    sums = jnp.dot(member.T, values, precision=highest)
    images, channels = sums.shape
    grouped = jnp.sum(sums.reshape(images, GROUPS, channels // GROUPS), axis=2) / counts[:, None]
    spread = jnp.repeat(grouped, channels // GROUPS, axis=1)
    return jnp.dot(member, spread, precision=highest)


def shards(
    features, heights, widths, timesteps, norm_gain, norm_shift, conv_weight, time_weight, cotangent
):
    rows, channels = features.shape
    replicas = lax.axis_size("dp")
    holders = lax.axis_size("fsdp")
    scale = 1.0 / math.sqrt(replicas * holders * rows)
    feature_count = time_weight.shape[1]
    heights_row = heights[0]
    widths_row = widths[0]
    neighbours, live, member = layout(heights_row, widths_row, rows)
    counts = jnp.maximum((heights_row * widths_row).astype(jnp.float32) * (channels // GROUPS), 1.0)
    values = features.astype(jnp.float32)
    mean = group_mean(values, member, counts)
    centered = values - mean
    variance = group_mean(centered * centered, member, counts)
    inverse_std = lax.rsqrt(variance + 1e-05) * live[:, None].astype(jnp.float32)
    normed = centered * inverse_std
    shifted = normed * norm_gain[None, :] + norm_shift[None, :]
    activated = (shifted * jax.nn.sigmoid(shifted)).astype(jnp.bfloat16)
    padded = jnp.concatenate([activated, jnp.zeros((1, channels), jnp.bfloat16)], axis=0)
    patches = padded[neighbours].reshape(rows, 9 * channels)
    cotan_live = jnp.where(live[:, None], cotangent, jnp.zeros_like(cotangent))
    cotan_padded = jnp.concatenate([cotan_live, jnp.zeros((1, CO), jnp.bfloat16)], axis=0)
    embed = timestep_features(timesteps[0], feature_count)
    conv_full, time_full = (
        lax.all_gather(conv_weight, "fsdp", axis=0, tiled=True),
        lax.all_gather(time_weight, "fsdp", axis=0, tiled=True),
    )
    bias_image = lax.dot_general(
        embed, time_full, (((1,), (1,)), ((), ())), preferred_element_type=jnp.float32
    )
    before = lax.dot_general(
        patches, conv_full, (((1,), (1,)), ((), ())), preferred_element_type=jnp.float32
    )
    before = before + jnp.dot(member, bias_image, precision=highest)
    block_out = jnp.where(live[:, None], before, 0.0).astype(jnp.bfloat16)
    reversed_taps = neighbours[:, ::-1]
    cotan_taps = cotan_padded[reversed_taps].reshape(rows, 9 * CO)
    tap_weight = conv_full.reshape(CO, 9, channels).transpose(1, 0, 2).reshape(9 * CO, channels)
    grad_act = jnp.dot(cotan_taps, tap_weight, preferred_element_type=jnp.float32)
    sigmoid_value = jax.nn.sigmoid(shifted)
    grad_shifted = grad_act * sigmoid_value * (1.0 + shifted * (1.0 - sigmoid_value))
    gain_term = jnp.sum(grad_shifted * normed, axis=0) * scale
    shift_term = jnp.sum(grad_shifted, axis=0) * scale
    grad_normed = grad_shifted * norm_gain[None, :]
    mean_grad = group_mean(grad_normed, member, counts)
    mean_cross = group_mean(grad_normed * normed, member, counts)
    grad_features = (inverse_std * (grad_normed - mean_grad - normed * mean_cross)).astype(
        jnp.bfloat16
    )
    per_image = jnp.dot(member.T, cotan_live.astype(jnp.float32), precision=highest)
    conv_part = lax.dot_general(
        cotan_live, patches, (((0,), (0,)), ((), ())), preferred_element_type=jnp.float32
    )
    time_part = lax.dot_general(
        per_image, embed.astype(jnp.float32), (((0,), (0,)), ((), ())), precision=highest
    )
    full_term = jnp.concatenate([conv_part, time_part], axis=1) * scale
    reduced = lax.psum_scatter(full_term, "fsdp", scatter_dimension=0, tiled=True)
    joined = lax.psum(reduced, "dp")
    grad_conv = joined[:, : 9 * channels]
    grad_time = joined[:, 9 * channels :]
    grad_gain, grad_shift = lax.psum((gain_term, shift_term), ("dp", "fsdp"))
    return (block_out, grad_features, grad_conv, grad_time, grad_gain, grad_shift)


def solution(mesh):
    placed = (
        P(("dp", "fsdp"), None),
        P(("dp", "fsdp"), None),
        P(("dp", "fsdp"), None),
        P(("dp", "fsdp"), None),
        P(),
        P(),
        P("fsdp", None),
        P("fsdp", None),
        P(("dp", "fsdp"), None),
    )
    return jax.shard_map(
        shards,
        mesh=mesh,
        in_specs=placed,
        out_specs=(
            P(("dp", "fsdp"), None),
            P(("dp", "fsdp"), None),
            P("fsdp", None),
            P("fsdp", None),
            P(),
            P(),
        ),
        check_vma=False,
    )
```

profile of v0, /device:TPU:4, one launch (start us, length us, event | category | flops | bytes accessed | tf_op | source)
XLA Modules:
  0.0 447.3 jit_solution(8211011394849279859)
XLA Ops:
  7.2 0.7 all-gather.2.cloned.1.call-update
  7.9 0.7 mul.425
  9.4 0.6 iota_compare_fusion.3
  10.1 0.8 select_reduce_fusion.2
  10.9 0.8 constant_dynamic-update-slice_fusion.8
  12.0 0.8 constant_dynamic-update-slice_fusion.5
  13.0 0.8 constant_dynamic-update-slice_fusion.2
  14.1 1.1 fusion.48
  16.1 0.7 multiply_maximum_fusion
  17.0 1.3 convolution_subtract_fusion.1
  19.1 0.7 fusion.45
  19.7 2.0 multiply_convert_fusion
  21.8 4.5 %gather_fusion = bf16[1152,640]{1,0:T(8,128)(2,1)S(1)} fusion(bf16[129,640]{1,0:T(8,128)(2,1)S(1)} %concatenate.32, s32[2048]{0:T(1024)S(1)} %get-tuple-element.44), kind=kCustom, calls=%fused_computation | custom fusion | bytes 2953728 | tf_op jit(solution)/shard_map/gather | solution.py:80
  26.3 1.7 reshape.1020
  28.4 0.9 fusion.41
  29.3 2.5 fusion.50
  31.8 7.5 %maximum_multiply_fusion = f32[768,6080]{1,0:T(8,128)} fusion(f32[768,320]{1,0:T(8,128)S(1)} %fusion.41, f32[768,5760]{1,0:T(8,128)S(1)} %fusion.50), kind=kLoop, calls=%fused_computation.2 | loop fusion | flops 9338880 | bytes 37355520 | tf_op jit(solution)/shard_map/mul | solution.py:117
  39.4 4.6 %gather_fusion.1 = bf16[1152,768]{1,0:T(8,128)(2,1)S(1)} fusion(bf16[129,768]{1,0:T(8,128)(2,1)S(1)} %concatenate.34, s32[2048]{0:T(1024)S(1)} %get-tuple-element.43), kind=kCustom, calls=%fused_computation.1 | custom fusion | bytes 3543552 | tf_op jit(solution)/shard_map/gather | solution.py:97
  43.9 2.4 reshape.1035
  46.4 42.6 %all_gather.7 = bf16[768,320]{1,0:T(8,128)(2,1)S(1)} all-gather(bf16[24,320]{1,0:T(8,128)(2,1)S(1)} %copy-done.4), channel_id=1, replica_groups=mesh['dp'=8,'fsdp'=32] {'fsdp'}, dimensions={0}, use_global_device_ids=true | all-gather | bytes 506880 | tf_op jit(solution)/shard_map/all_gather | solution.py:86
  89.2 28.9 %all-gather.2.cloned.1.call-done = bf16[768,5760]{1,0:T(8,128)(2,1)} async-done(((bf16[24,5760]{1,0:T(8,128)(2,1)}), bf16[768,5760]{1,0:T(8,128)(2,1)}) %all-gather.2.cloned.1.call-update) | async-done | bytes 8847376 | tf_op jit(solution)/shard_map/all_gather | solution.py:85
  118.1 11.8 %copy.31 = bf16[768,5760]{0,1:T(8,128)(2,1)} copy(bf16[768,5760]{1,0:T(8,128)(2,1)} %all-gather.2.cloned.1.call-done) | data formatting | bytes 17694720 | tf_op jit(solution)/shard_map/all_gather | solution.py:85
  129.9 13.7 %copy.32 = bf16[768,9,640]{2,0,1:T(8,128)(2,1)} copy(bf16[768,9,640]{0,2,1:T(8,128)(2,1)} %bitcast.252) | data formatting | bytes 17694720 | tf_op jit(solution)/shard_map/reshape | solution.py:98
  143.6 7.8 %fusion.46 = (f32[640]{0:T(1024)S(1)}, f32[640]{0:T(1024)S(1)}, f32[128,640]{1,0:T(8,128)S(1)}) fusion(f32[128,640]{1,0:T(8,128)S(1)} %copy-done, f32[640]{0:T(1024)S(1)} %copy-done.5, f32[640]{0:T(1024)S(1)} %copy-done.3, bf16[768,9,640]{2,0,1:T(8,128)(2,1)} %copy.32, bf16[128,9,768]{2,1,0:T(8,128)(2,1)} %reshape.1035), kind=kOutput, calls=%fused_computation.108 | convolution fusion | flops 1133525760 | bytes 11282432 | tf_op jit(solution)/shard_map/dot_general | solution.py:99
  152.4 7.1 %fusion.49 = f32[128,768]{1,0:T(8,128)S(1)} fusion(bf16[128,5760]{1,0:T(8,128)(2,1)S(1)} %reshape.1020, bf16[768,5760]{1,0:T(8,128)(2,1)} %all-gather.2.cloned.1.call-done), kind=kOutput, calls=%fused_computation.110 | convolution fusion | flops 1132462080 | bytes 10715136 | tf_op jit(solution)/shard_map/dot_general | solution.py:91
  159.5 1.1 fusion.13
  160.6 192.4 %reduce-scatter.2.cloned.1.call-done = f32[24,6080]{1,0:T(8,128)} async-done(((f32[768,6080]{1,0:T(8,128)}), f32[24,6080]{1,0:T(8,128)}) %reduce-scatter.2.cloned.1.call-update) | async-done | bytes 583696 | tf_op jit(solution)/shard_map/reduce_scatter | solution.py:118
  353.5 75.8 %all-reduce.2 = (f32[640]{0:T(1024)}, f32[640]{0:T(1024)}) all-reduce(f32[640]{0:T(1024)S(1)} %broadcast_multiply_fusion.1, f32[640]{0:T(1024)S(1)} %broadcast_multiply_fusion), channel_id=1, replica_groups=mesh['dp'=8,'fsdp'=32] {'dp','fsdp'}, use_global_device_ids=true, to_apply=%region_12.13 | all-reduce | flops 1280 | bytes 10240 | tf_op jit(solution)/shard_map/psum | solution.py:122
  429.7 1.1 fusion.24
  430.7 6.8 %all-reduce.5.cloned.1.call-done = f32[24,6080]{1,0:T(8,128)} async-done(((f32[24,6080]{1,0:T(8,128)}), f32[24,6080]{1,0:T(8,128)}) %all-reduce.5.cloned.1.call-update) | async-done | bytes 583696 | tf_op jit(solution)/shard_map/psum | solution.py:119
  437.5 1.4 slice.18
  438.9 1.9 slice.17
  (71 shorter events, 6.2 us)
Async XLA Ops:
  7.2 110.9 %all-gather.2.cloned.1.call-start = ((), (), s32[]{:S(2)}) async-start(), calls=%async_computation.1 | async-start | bytes 9123840 | tf_op jit(solution)/shard_map/all_gather | solution.py:85
  7.9 345.1 %reduce-scatter.2.cloned.1.call-start = ((), (), s32[]{:S(2)}) async-start(), calls=%async_computation.2 | async-start | bytes 19464192 | tf_op jit(solution)/shard_map/reduce_scatter | solution.py:118
  21.7 6.3 %copy-start.6 = (s32[1,4]{1,0:T(1,128)S(1)}, s32[1,4]{1,0:T(1,128)}, u32[]{:S(2)}) copy-start(s32[1,4]{1,0:T(1,128)} %param.12) | copy-start | bytes 52
  21.8 6.4 %copy-start.2 = (bf16[128,768]{1,0:T(8,128)(2,1)S(1)}, bf16[128,768]{1,0:T(8,128)(2,1)}, u32[]{:S(2)}) copy-start(bf16[128,768]{1,0:T(8,128)(2,1)} %param.17) | copy-start | bytes 589828
  39.3 398.3 %all-reduce.5.cloned.1.call-start = ((), (), s32[]{:S(2)}) async-start(), calls=%async_computation.3 | async-start | bytes 1179648 | tf_op jit(solution)/shard_map/psum | solution.py:119
  43.9 2.5 copy-start.4
  129.9 13.7 %copy-start = (f32[128,640]{1,0:T(8,128)S(1)}, f32[128,640]{1,0:T(8,128)}, u32[]{:S(2)}) copy-start(f32[128,640]{1,0:T(8,128)} %get-tuple-element.36) | copy-start | bytes 983044
  129.9 13.7 %copy-start.3 = (f32[640]{0:T(1024)S(1)}, f32[640]{0:T(1024)}, u32[]{:S(2)}) copy-start(f32[640]{0:T(1024)} %param.13) | copy-start | bytes 7684
  129.9 13.7 %copy-start.5 = (f32[640]{0:T(1024)S(1)}, f32[640]{0:T(1024)}, u32[]{:S(2)}) copy-start(f32[640]{0:T(1024)} %param.14) | copy-start | bytes 7684
  152.4 277.3 %copy-start.1 = (f32[128,640]{1,0:T(8,128)S(1)}, f32[128,640]{1,0:T(8,128)}, u32[]{:S(2)}) copy-start(f32[128,640]{1,0:T(8,128)} %get-tuple-element.41) | copy-start | bytes 983044
Sparse Core Ops, SparseCore 0:
  10.8 107.2 all-gather.1
  122.7 230.2 reduce-scatter.1
  355.7 81.8 all-reduce.4
where the time goes:
time: 449 us; the launch traced here: 447 us
  waiting for transfers between devices  229 us (51%)
  blocking collectives  118 us (26%)
  local copies, waits for them, and re-layouts  44.7 us (10%)
  matrix products  26.2 us (6%)
  other arithmetic  15.2 us (3%)
  between operations  14 us (3%)
    reduce_scatter x1, waiting for transfers between devices, shards(): lax.psum_scatter(full_term, 'fsdp', scatter_dimension=0, tiled=True)  192 us
    psum x1, blocking collectives, shards(): grad_gain, grad_shift = lax.psum((gain_term, shift_term), ('dp', 'fsdp'))  75.8 us
    all_gather x1, blocking collectives, shards(): lax.all_gather(time_weight, 'fsdp', axis=0, tiled=True)  42.6 us
    all_gather x1, waiting for transfers between devices, shards(): lax.all_gather(conv_weight, 'fsdp', axis=0, tiled=True)  28.9 us
    reshape x1, local copies, waits for them, and re-layouts, shards(): conv_full.reshape(CO, 9, channels).transpose(1, 0, 2)  13.7 us
    all_gather x1, local copies, waits for them, and re-layouts, shards(): lax.all_gather(conv_weight, 'fsdp', axis=0, tiled=True)  11.8 us
  transfers between devices with their start and end apart: 3, of which 3 were waited for; matrix products, arithmetic and copies ran while one was open for 18% of the time, Pallas kernels for 0%

commit v1 on v0

v1 whole, which is shorter than its diff:
```python
import functools
import math

import jax
import jax.numpy as jnp
from jax import lax
from jax.experimental import pallas as pl
from jax.experimental.pallas import tpu as pltpu
from jax.sharding import PartitionSpec as P

GROUPS = 32
TAP_ROWS = 16
EXTRA = 8
TIME_WIDTH = 384

highest = lax.Precision.HIGHEST


def layout(heights, widths, rows):
    images = heights.shape[1]
    area = heights * widths
    position = jnp.arange(rows, dtype=jnp.int32)[None, :]
    first = jnp.zeros((heights.shape[0], rows), jnp.int32)
    height = first
    width = first
    begin = jnp.zeros((heights.shape[0],), jnp.int32)
    members = []
    for image in range(images):
        end = begin + area[:, image]
        member = (position >= begin[:, None]) & (position < end[:, None])
        members.append(member)
        first = jnp.where(member, begin[:, None], first)
        height = jnp.where(member, heights[:, image, None], height)
        width = jnp.where(member, widths[:, image, None], width)
        begin = end
    live = position < begin[:, None]
    offset = position - first
    width_safe = jnp.maximum(width, 1)
    row_index = offset // width_safe
    column = offset - row_index * width_safe
    targets = []
    for shift_row in (-1, 0, 1):
        for shift_col in (-1, 0, 1):
            near_row = row_index + shift_row
            near_col = column + shift_col
            valid = (
                live & (near_row >= 0) & (near_row < height) & (near_col >= 0) & (near_col < width)
            )
            targets.append(jnp.where(valid, first + near_row * width + near_col, rows))
    targets += [jnp.full_like(first, rows)] * (TAP_ROWS - len(targets))
    return jnp.stack(targets, axis=1), live, jnp.stack(members, axis=1).astype(jnp.float32)


def timestep_features(times, feature_count):
    half = feature_count // 2
    rates = jnp.exp(-math.log(10000.0) * jnp.arange(half, dtype=jnp.float32) / half)
    angles = times.astype(jnp.float32)[:, None] * rates[None, :]
    return jnp.concatenate([jnp.sin(angles), jnp.cos(angles)], axis=1).astype(jnp.bfloat16)


def group_mean(values, member, counts):
    sums = jnp.dot(member.T, values, precision=highest)
    images, channels = sums.shape
    grouped = jnp.sum(sums.reshape(images, GROUPS, channels // GROUPS), axis=2) / counts[:, None]
    spread = jnp.repeat(grouped, channels // GROUPS, axis=1)
    return jnp.dot(member, spread, precision=highest)


def dot32(left, right, dims):
    return lax.dot_general(left, right, (dims, ((), ())), preferred_element_type=jnp.float32)


def conv_kernel(taps, act_ref, cot_ref, near_ref, order_ref, embed_ref, mine_ref, other_ref,
                mine_time_ref, other_time_ref, out_ref, grad_ref, cot_sc, out_sc):
    tap = pl.program_id(0)
    rows = act_ref.shape[0]
    half = mine_ref.shape[0]

    @pl.when(tap == 0)
    def _():
        cot_sc[...] = dot32(cot_ref[...], order_ref[...], ((1,), (0,))).astype(jnp.bfloat16)
        out_sc[:, :half] = dot32(embed_ref[...], mine_time_ref[...], ((1,), (1,)))
        out_sc[:, half:] = dot32(embed_ref[...], other_time_ref[...], ((1,), (1,)))
        grad_ref[...] = jnp.zeros_like(grad_ref)

    target = lax.broadcasted_iota(jnp.int32, (rows, rows), 0)
    pick = (near_ref[pl.ds(taps - 1 - tap, 1), :] == target).astype(jnp.float32).astype(jnp.bfloat16)
    back = (near_ref[pl.ds(tap, 1), :] == target).astype(jnp.float32).astype(jnp.bfloat16)
    patch = dot32(pick, act_ref[...], ((1,), (0,))).astype(jnp.bfloat16)
    shifted_cot = dot32(back, cot_sc[...], ((1,), (0,))).astype(jnp.bfloat16)
    mine = mine_ref[...]
    other = other_ref[...]
    out_sc[:, :half] += dot32(patch, mine, ((1,), (1,)))
    out_sc[:, half:] += dot32(patch, other, ((1,), (1,)))
    grad_ref[...] += dot32(shifted_cot[:, :half], mine, ((1,), (0,))) + dot32(
        shifted_cot[:, half:], other, ((1,), (0,))
    )

    @pl.when(tap == taps - 1)
    def _():
        rounded = out_sc[...].astype(jnp.bfloat16)
        out_ref[...] = dot32(rounded, order_ref[...], ((1,), (1,))).astype(jnp.bfloat16)


def conv_both(act, cot, near, order, embed, mine, other, taps):
    rows, channels = act.shape
    outs = cot.shape[1]
    half = mine.shape[0]
    tail = taps * channels // TIME_WIDTH
    whole = lambda shape: pl.BlockSpec(shape, lambda t: (0, 0))
    return pl.pallas_call(
        functools.partial(conv_kernel, taps),
        grid=(taps,),
        in_specs=[
            whole((rows, channels)),
            whole((rows, outs)),
            whole((TAP_ROWS, rows)),
            whole((outs, outs)),
            whole((rows, TIME_WIDTH)),
            pl.BlockSpec((half, channels), lambda t: (0, t)),
            pl.BlockSpec((half, channels), lambda t: (0, t)),
            pl.BlockSpec((half, TIME_WIDTH), lambda t: (0, tail)),
            pl.BlockSpec((half, TIME_WIDTH), lambda t: (0, tail)),
        ],
        out_specs=[whole((rows, outs)), whole((rows, channels))],
        out_shape=[
            jax.ShapeDtypeStruct((rows, outs), jnp.bfloat16),
            jax.ShapeDtypeStruct((rows, channels), jnp.float32),
        ],
        scratch_shapes=[
            pltpu.VMEM((rows, outs), jnp.bfloat16),
            pltpu.VMEM((rows, outs), jnp.float32),
        ],
        cost_estimate=pl.CostEstimate(
            flops=4 * rows * outs * channels * taps,
            bytes_accessed=2 * outs * channels * taps,
            transcendentals=0,
        ),
        name="conv_both",
    )(act, cot, near, order, embed, mine, other, mine, other)


def weight_kernel(taps, owned, scale, side_ref, near_ref, cot_ref, mine_ref, other_ref, time_ref,
                  out_ref, acc):
    step = pl.program_id(0)
    pairs, rows, channels = mine_ref.shape

    @pl.when(step == 0)
    def _():
        acc[...] = jnp.zeros_like(acc)

    source = lax.broadcasted_iota(jnp.int32, (rows, rows), 0)
    side = side_ref[0]
    pieces = []
    acts = []
    for pair in range(pairs):
        for act_ref, core in ((mine_ref, side), (other_ref, 1 - side)):
            near = near_ref[pair, core]
            cot = cot_ref[pair, core]
            parts = []
            for tap in range(taps):
                other_tap = taps - 1 - tap
                pick = (near[other_tap : other_tap + 1, :] == source).astype(jnp.float32)
                parts.append(dot32(cot, pick.astype(jnp.bfloat16), ((1,), (0,)))[:owned, :])
            pieces.append(jnp.concatenate(parts, axis=0).astype(jnp.bfloat16))
            acts.append(act_ref[pair])
    acc[...] += dot32(
        jnp.concatenate(pieces, axis=1), jnp.concatenate(acts, axis=0), ((1,), (0,))
    )

    @pl.when(step == pl.num_programs(0) - 1)
    def _():
        out_ref[:, taps * channels :] = time_ref[...]
        for tap in range(taps):
            out_ref[:, tap * channels : (tap + 1) * channels] = (
                acc[tap * owned : (tap + 1) * owned, :] * scale
            )


def weight_grad(side, near, cot, mine, other, time_part, taps, owned, scale):
    half, rows, channels = mine.shape
    pairs = 2
    deep = cot.shape[2]
    return pl.pallas_call(
        functools.partial(weight_kernel, taps, owned, scale),
        grid_spec=pltpu.PrefetchScalarGridSpec(
            num_scalar_prefetch=1,
            grid=(half // pairs,),
            in_specs=[
                pl.BlockSpec((pairs, 2, TAP_ROWS, rows), lambda g, s: (g, 0, 0, 0)),
                pl.BlockSpec((pairs, 2, deep, rows), lambda g, s: (g, 0, 0, 0)),
                pl.BlockSpec((pairs, rows, channels), lambda g, s: (g, 0, 0)),
                pl.BlockSpec((pairs, rows, channels), lambda g, s: (g, 0, 0)),
                pl.BlockSpec((owned, TIME_WIDTH), lambda g, s: (0, 0)),
            ],
            out_specs=pl.BlockSpec((owned, taps * channels + TIME_WIDTH), lambda g, s: (0, 0)),
            scratch_shapes=[pltpu.VMEM((taps * owned, channels), jnp.float32)],
        ),
        out_shape=jax.ShapeDtypeStruct((owned, taps * channels + TIME_WIDTH), jnp.float32),
        cost_estimate=pl.CostEstimate(
            flops=4 * half * rows * channels * taps * owned,
            bytes_accessed=4 * half * rows * channels,
            transcendentals=0,
        ),
        name="weight_grad",
    )(side, near, cot, mine, other, time_part)


def gather_half(block, holders):
    groups = [list(range(core, holders, 2)) for core in (0, 1)]
    return lax.all_gather(block, "fsdp", axis=0, tiled=True, axis_index_groups=groups)


def from_partner(block, holders):
    return lax.ppermute(block, "fsdp", [(i, i ^ 1) for i in range(holders)])


def shards(
    features, heights, widths, timesteps, norm_gain, norm_shift, conv_weight, time_weight, cotangent
):
    rows, channels = features.shape
    images = heights.shape[1]
    outs = cotangent.shape[1]
    owned = conv_weight.shape[0]
    taps = conv_weight.shape[1] // channels
    replicas = lax.axis_size("dp")
    holders = lax.axis_size("fsdp")
    scale = 1.0 / math.sqrt(replicas * holders * rows)
    feature_count = time_weight.shape[1]
    side = lax.axis_index("fsdp") % 2

    both = jnp.concatenate(
        [conv_weight, time_weight, jnp.zeros((owned, TIME_WIDTH - feature_count), jnp.bfloat16)],
        axis=1,
    )
    mine = gather_half(both, holders)

    near_all, live_all, member_all = layout(heights, widths, rows)
    near, live, member = near_all[0], live_all[0], member_all[0].T
    cotan_live = jnp.where(live[:, None], cotangent, jnp.zeros_like(cotangent))

    facts = jnp.concatenate(
        [heights[0], widths[0], timesteps[0] // 32, timesteps[0] % 32]
    ).astype(jnp.bfloat16)
    facts = jnp.pad(facts[None, :], ((0, EXTRA - 1), (0, rows - facts.shape[0])))
    columns = cotan_live.T.reshape(holders, owned, rows)
    packed = jnp.concatenate(
        [columns, jnp.broadcast_to(facts[None], (holders, EXTRA, rows))], axis=1
    )
    swapped = lax.all_to_all(packed, "fsdp", 0, 0, tiled=True)

    counts = jnp.maximum((heights[0] * widths[0]).astype(jnp.float32) * (channels // GROUPS), 1.0)
    values = features.astype(jnp.float32)
    mean = group_mean(values, member, counts)
    centered = values - mean
    variance = group_mean(centered * centered, member, counts)
    inverse_std = lax.rsqrt(variance + 1e-05) * live[:, None].astype(jnp.float32)
    normed = centered * inverse_std
    shifted = normed * norm_gain[None, :] + norm_shift[None, :]
    sigmoid_value = jax.nn.sigmoid(shifted)
    activated = (shifted * sigmoid_value).astype(jnp.bfloat16)
    act_mine = gather_half(activated, holders)

    told = swapped[:, owned, : 4 * images].astype(jnp.int32)
    group_near, _, group_member = layout(told[:, :images], told[:, images : 2 * images], rows)
    group_times = told[:, 2 * images : 3 * images] * 32 + told[:, 3 * images :]
    group_embed = timestep_features(group_times.reshape(-1), feature_count)
    per_image = jnp.einsum(
        "bmr,bor->bmo", group_member, swapped[:, :owned].astype(jnp.float32), precision=highest
    ).reshape(holders * images, owned)
    time_part = jnp.dot(per_image.T, group_embed.astype(jnp.float32), precision=highest) * scale
    near_flat = group_near.reshape(holders // 2, 2, TAP_ROWS, rows)
    mine, near_flat, time_part = lax.optimization_barrier((mine, near_flat, time_part))
    other = from_partner(mine, holders)

    embed = timestep_features(timesteps[0], feature_count)
    embed_rows = jnp.dot(member, embed.astype(jnp.float32), precision=highest).astype(jnp.bfloat16)
    embed_rows = jnp.pad(embed_rows, ((0, 0), (0, TIME_WIDTH - feature_count)))
    natural = jnp.arange(outs, dtype=jnp.int32)
    slot = (natural // (2 * owned)) * owned + natural % owned
    slot = slot + jnp.where((natural // owned) % 2 == side, 0, outs // 2)
    order = (slot[:, None] == natural[None, :]).astype(jnp.bfloat16)
    block_out, grad_act = conv_both(activated, cotan_live, near, order, embed_rows, mine, other, taps)
    act_mine, grad_act = lax.optimization_barrier((act_mine, grad_act))
    act_other = from_partner(act_mine, holders)

    grad_shifted = grad_act * sigmoid_value * (1.0 + shifted * (1.0 - sigmoid_value))
    gain_term = jnp.sum(grad_shifted * normed, axis=0) * scale
    shift_term = jnp.sum(grad_shifted, axis=0) * scale
    grad_normed = grad_shifted * norm_gain[None, :]
    mean_grad = group_mean(grad_normed, member, counts)
    mean_cross = group_mean(grad_normed * normed, member, counts)
    grad_features = (inverse_std * (grad_normed - mean_grad - normed * mean_cross)).astype(
        jnp.bfloat16
    )

    parts = weight_grad(
        side.astype(jnp.int32)[None],
        near_flat,
        swapped.reshape(holders // 2, 2, owned + EXTRA, rows),
        act_mine.reshape(holders // 2, rows, channels),
        act_other.reshape(holders // 2, rows, channels),
        jnp.pad(time_part, ((0, 0), (0, TIME_WIDTH - feature_count))),
        taps,
        owned,
        scale,
    )
    parts, gain_term, shift_term = lax.optimization_barrier((parts, gain_term, shift_term))
    joined = lax.psum(parts, "dp")
    grad_gain, grad_shift = lax.psum((gain_term, shift_term), ("dp", "fsdp"))
    grad_conv = joined[:, : taps * channels]
    grad_time = joined[:, taps * channels : taps * channels + feature_count]
    return (block_out, grad_features, grad_conv, grad_time, grad_gain, grad_shift)


def solution(mesh):
    rows = P(("dp", "fsdp"), None)
    held = P("fsdp", None)
    return jax.shard_map(
        shards,
        mesh=mesh,
        in_specs=(rows, rows, rows, rows, P(), P(), held, held, rows),
        out_specs=(rows, rows, held, held, P(), P()),
        check_vma=False,
    )
```

time: 449 us -> 324 us (0.72)
  waiting for transfers between devices: 229 us -> 144 us
  blocking collectives: 118 us -> 76.8 us
  local copies, waits for them, and re-layouts: 44.7 us -> 22.8 us
  Pallas kernels: 0 us -> 21.4 us
  matrix products: 26.2 us -> 9.96 us
  starting transfers between devices: 0.12 us -> 11.7 us
    reduce_scatter x1 -> x0, waiting for transfers between devices: 192 us -> none  [shards(): lax.psum_scatter(full_term, 'fsdp', scatter_dimension=0, tiled=True)]
    all_gather x1 -> x2, waiting for transfers between devices: 28.9 us -> 137 us  [gather_half(): lax.all_gather(block, 'fsdp', axis=0, tiled=True, axis_index_groups=groups)]
    all_gather x1 -> x0, blocking collectives: 42.6 us -> none  [shards(): lax.all_gather(time_weight, 'fsdp', axis=0, tiled=True)]
    pallas_call x0 -> x2, Pallas kernels: none -> 21.4 us  [the longest x1 12.5 us: conv_both(): pl.pallas_call(functools.partial(conv_kernel, taps), grid=(taps,), in_spe...]
    dot_general x7 -> x3, matrix products: 19.7 us -> 1.41 us  [the longest x1 0.9 us: shards(): jnp.dot(per_image.T, group_embed.astype(jnp.float32), precision=highest)]
    reshape x6 -> x0, local copies, waits for them, and re-layouts: 15.9 us -> none  [the longest x1 13.7 us: shards(): conv_full.reshape(CO, 9, channels).transpose(1, 0, 2)]
    all_gather x1 -> x0, local copies, waits for them, and re-layouts: 11.8 us -> none  [shards(): lax.all_gather(conv_weight, 'fsdp', axis=0, tiled=True)]
    all_to_all x0 -> x1, starting transfers between devices: none -> 11.6 us  [shards(): swapped = lax.all_to_all(packed, 'fsdp', 0, 0, tiled=True)]
  transfers between devices with their start and end apart: 3 -> 6, of which waited for: 3 -> 5; matrix products, arithmetic and copies ran while one was open for 18% -> 14% of each run, Pallas kernels for 0% -> 4%
where the time goes in v1:
time: 324 us; the launch traced here: 322 us
  waiting for transfers between devices  144 us (44%)
  blocking collectives  76.8 us (24%)
  local copies, waits for them, and re-layouts  22.8 us (7%)
  Pallas kernels  21.4 us (7%)
  other arithmetic  18.6 us (6%)
  between operations  16.7 us (5%)
  starting transfers between devices  11.7 us (4%)
  matrix products  9.96 us (3%)
    all_gather x2, waiting for transfers between devices, gather_half(): lax.all_gather(block, 'fsdp', axis=0, tiled=True, axis_index_groups=groups)  137 us
    psum x1, blocking collectives, shards(): grad_gain, grad_shift = lax.psum((gain_term, shift_term), ('dp', 'fsdp'))  76.8 us
    pallas_call x1, Pallas kernels, conv_both(): pl.pallas_call(functools.partial(conv_kernel, taps), grid=(taps,), in_spe...  12.5 us
    all_to_all x1, starting transfers between devices, shards(): swapped = lax.all_to_all(packed, 'fsdp', 0, 0, tiled=True)  11.6 us
    pallas_call x1, Pallas kernels, weight_grad(): pl.pallas_call(functools.partial(weight_kernel, taps, owned, scale), grid...  8.87 us
    select_n x6, other arithmetic, layout(): targets.append(jnp.where(valid, first + near_row * width + near_col, rows))  7.95 us
    dot_general x8, local copies, waits for them, and re-layouts, group_mean(): sums = jnp.dot(member.T, values, precision=highest)  7.59 us
  transfers between devices with their start and end apart: 6, of which 5 were waited for; matrix products, arithmetic and copies ran while one was open for 14% of the time, Pallas kernels for 4%

profile of v1, /device:TPU:4, one launch (start us, length us, event | category | flops | bytes accessed | tf_op | source)
XLA Modules:
  0.0 321.8 jit_solution(439086005940347774)
XLA Ops:
  7.3 1.8 concatenate.27
  14.3 1.0 fusion.95
  17.0 11.6 %all-to-all-start = ((bf16[32,32,128]{2,1,0:T(8,128)(2,1)}), bf16[32,32,128]{2,1,0:T(8,128)(2,1)S(1)}, u32[]{:S(2)}, u32[]{:S(2)}) async-start(bf16[32,32,128]{2,1,0:T(8,128)(2,1)} %pad_maximum_fusion), calls=%async_computation | async-start | bytes 524288 | tf_op jit(solution)/shard_map/all_to_all | solution.py:250
  30.9 5.6 %and_select_fusion.12 = (s32[1,1,128]{2,1,0:T(1,128)S(1)}, s32[1,1,128]{2,1,0:T(1,128)S(1)}, pred[1,1,128]{2,1,0:T(4,128)(4,1)S(1)}, s32[1,1,128]{2,1,0:T(1,128)...) fusion(s32[]{:T(128)} %bitcast.3, s32[]{:T(128)} %bitcast.12, ...), kind=kLoop, calls=%fused_computation.164 | loop fusion | flops 6144 | bytes 4144 | tf_op jit(solution)/shard_map/jit(_where)/select_n | solution.py:49
  37.8 0.8 convolution_reduce_fusion.2
  38.9 3.8 %all-to-all-done = bf16[32,32,128]{2,1,0:T(8,128)(2,1)S(1)} async-done(((bf16[32,32,128]{2,1,0:T(8,128)(2,1)}), bf16[32,32,128]{2,1,0:T(8,128)(2,1)S(1)}, u32[]{:S(2)}, u32[]{:S(2)}) %all-to-all-start) | async-done | bytes 262176 | tf_op jit(solution)/shard_map/all_to_all | solution.py:250
  44.5 1.9 and_select_fusion
  46.8 1.6 stack.22.near_ref
  49.2 0.9 convolution_multiply_fusion.1
  50.1 68.3 %all-gather.3.cloned.1.call-done.mine_ref.mine_time_ref = bf16[384,6144]{1,0:T(8,128)(2,1)} async-done(((bf16[24,6144]{1,0:T(8,128)(2,1)}), bf16[384,6144]{1,0:T(8,128)(2,1)}) %all-gather.3.cloned.1.call-update) | async-done | bytes 4718608 | tf_op jit(solution)/shard_map/all_gather | solution.py:211
  118.5 1.2 multiply_convert_fusion
  121.0 1.2 stack.19
  122.3 0.8 broadcast_select_fusion.cot_ref
  123.1 1.3 fusion.order_ref
  124.4 2.3 collective-permute-done.other_ref.other_time_ref
  126.7 12.5 %conv_both.1 = (bf16[128,768]{1,0:T(8,128)(2,1)}, f32[128,640]{1,0:T(8,128)}) custom-call(bf16[128,640]{1,0:T(8,128)(2,1)} %get-tuple-element.73.act_ref, bf16[128,768]{1,0:T(8,128)(2,1)} %broadcast_select_fusion.cot_ref, s32[16,128]{1,0:T(8,128)} %bitcast.68, bf16[768,768]{1,0:T(8,128)(2,1)} %fusion.order_ref, bf16[128,384]{1,0:T(8,128)(2,1)} %pad.12.embed_ref, ...), custom_call_target="tpu_custom_call" | custom-call | flops 2264924160 | bytes 8847360 | tf_op jit(solution)/shard_map/conv_both/pallas_call | solution.py:111
  139.2 68.4 %all-gather.5.cloned.1.call-done = bf16[2048,640]{1,0:T(8,128)(2,1)} async-done(((bf16[128,640]{1,0:T(8,128)(2,1)}), bf16[2048,640]{1,0:T(8,128)(2,1)}) %all-gather.5.cloned.1.call-update) | async-done | bytes 2621456 | tf_op jit(solution)/shard_map/all_gather | solution.py:211
  208.2 1.1 fusion.84
  209.4 0.9 multiply_bitcast_fusion.2
  210.3 1.9 copy.39
  212.1 1.7 dot_general.65
  213.9 1.9 copy.37
  215.7 1.7 dot_general.61
  217.5 1.8 convolution_reduce_fusion
  219.2 1.8 convolution_reduce_fusion.1
  221.0 1.5 copy-done
  222.5 8.9 %weight_grad.1 = f32[24,6144]{1,0:T(8,128)} custom-call(s32[1]{0:T(128)} %bitcast.25.side_ref, s32[16,2,16,128]{3,2,1,0:T(8,128)} %stack.22.near_ref, bf16[16,2,32,128]{3,2,1,0:T(8,128)(2,1)} %bitcast.64, bf16[16,128,640]{2,1,0:T(8,128)(2,1)} %bitcast.62, bf16[16,128,640]{2,1,0:T(8,128)(2,1)} %bitcast.63, f32[24,384]{1,0:T(8,128)} %pad.14.time_ref), custom_call_target="tpu_custom_call" | custom-call | flops 1132462080 | bytes 5242880 | tf_op jit(solution)/shard_map/weight_grad/pallas_call | solution.py:184
  232.2 2.0 fusion.5
  234.3 76.8 %all-reduce.3 = (f32[640]{0:T(1024)}, f32[640]{0:T(1024)}) all-reduce(f32[640]{0:T(1024)S(1)} %get-tuple-element.24, f32[640]{0:T(1024)S(1)} %get-tuple-element.25), channel_id=1, replica_groups=mesh['dp'=8,'fsdp'=32] {'dp','fsdp'}, use_global_device_ids=true, to_apply=%region_7.8 | all-reduce | flops 1280 | bytes 10240 | tf_op jit(solution)/shard_map/psum | solution.py:310
  311.1 0.9 all-reduce.6.cloned.1.call-done
  312.0 1.9 slice.157
  313.9 1.4 slice.158
  (99 shorter events, 14.0 us)
Async XLA Ops:
  7.2 23.0 %copy-start.7 = (s32[1,4]{1,0:T(1,128)S(1)}, s32[1,4]{1,0:T(1,128)}, u32[]{:S(2)}) copy-start(s32[1,4]{1,0:T(1,128)} %param.10) | copy-start | bytes 52
  7.2 22.4 %copy-start.6 = (s32[1,4]{1,0:T(1,128)S(1)}, s32[1,4]{1,0:T(1,128)}, u32[]{:S(2)}) copy-start(s32[1,4]{1,0:T(1,128)} %param.11) | copy-start | bytes 52
  7.2 21.5 %copy-start.3 = (bf16[128,640]{1,0:T(8,128)(2,1)S(1)}, bf16[128,640]{1,0:T(8,128)(2,1)}, u32[]{:S(2)}) copy-start(bf16[128,640]{1,0:T(8,128)(2,1)} %param.9) | copy-start | bytes 491524
  7.2 111.3 %all-gather.3.cloned.1.call-start = ((), (), s32[]{:S(2)}) async-start(), calls=%async_computation.1 | async-start | bytes 5013504 | tf_op jit(solution)/shard_map/all_gather | solution.py:211
  17.0 25.6 %all-to-all-start = ((bf16[32,32,128]{2,1,0:T(8,128)(2,1)}), bf16[32,32,128]{2,1,0:T(8,128)(2,1)S(1)}, u32[]{:S(2)}, u32[]{:S(2)}) async-start(bf16[32,32,128]{2,1,0:T(8,128)(2,1)} %pad_maximum_fusion), calls=%async_computation | async-start | bytes 524288 | tf_op jit(solution)/shard_map/all_to_all | solution.py:250
  28.6 179.0 %all-gather.5.cloned.1.call-start = ((), (), s32[]{:S(2)}) async-start(), calls=%async_computation.2 | async-start | bytes 2785280 | tf_op jit(solution)/shard_map/all_gather | solution.py:211
  37.5 80.9 %copy-start.5 = (f32[640]{0:T(1024)S(1)}, f32[640]{0:T(1024)}, u32[]{:S(2)}) copy-start(f32[640]{0:T(1024)} %param.13) | copy-start | bytes 7684
  37.5 80.9 %copy-start.8 = (f32[640]{0:T(1024)S(1)}, f32[640]{0:T(1024)}, u32[]{:S(2)}) copy-start(f32[640]{0:T(1024)} %param.14) | copy-start | bytes 7684
  42.6 78.4 %copy-start.1 = (bf16[32,32,128]{2,1,0:T(8,128)(2,1)}, bf16[32,32,128]{2,1,0:T(8,128)(2,1)S(1)}, u32[]{:S(2)}) copy-start(bf16[32,32,128]{2,1,0:T(8,128)(2,1)S(1)} %all-to-all-done) | copy-start | bytes 786436
  42.7 79.6 %copy-start.2 = (bf16[128,768]{1,0:T(8,128)(2,1)S(1)}, bf16[128,768]{1,0:T(8,128)(2,1)}, u32[]{:S(2)}) copy-start(bf16[128,768]{1,0:T(8,128)(2,1)} %param.17) | copy-start | bytes 589828
  118.5 8.3 %collective-permute-start = (bf16[384,6144]{1,0:T(8,128)(2,1)}, bf16[384,6144]{1,0:T(8,128)(2,1)}, u32[]{:S(2)}, u32[]{:S(2)}) collective-permute-start(bf16[384,6144]{1,0:T(8,128)(2,1)} %all-gather.3.cloned.1.call-done.mine_ref.mine_time_ref), channel_id=1, source_target_pairs={{0,1},{1,0},{2,3},{3,2},{4,5},{5,4},{6,7},{7,6},{8,9},{9,8},{10,11... | collective-permute-start | bytes 14155784 | tf_op jit(solution)/shard_map/ppermute | solution.py:215
  119.7 192.3 %all-reduce.6.cloned.1.call-start = ((), (), s32[]{:S(2)}) async-start(), calls=%async_computation.3 | async-start | bytes 1179648 | tf_op jit(solution)/shard_map/psum | solution.py:309
  126.7 80.9 %copy-start.4 = (f32[24,320]{1,0:T(8,128)S(1)}, f32[24,320]{1,0:T(8,128)}, u32[]{:S(2)}) copy-start(f32[24,320]{1,0:T(8,128)} %convolution_multiply_fusion.1) | copy-start | bytes 92164
  207.6 13.4 %collective-permute-start.1 = (bf16[2048,640]{1,0:T(8,128)(2,1)}, bf16[2048,640]{1,0:T(8,128)(2,1)S(1)}, u32[]{:S(2)}, u32[]{:S(2)}) collective-permute-start(bf16[2048,640]{1,0:T(8,128)(2,1)} %all-gather.5.cloned.1.call-done), channel_id=1, source_target_pairs={{0,1},{1,0},{2,3},{3,2},{4,5},{5,4},{6,7},{7,6},{8,9},{9,8},{10,11... | collective-permute-start | bytes 7864328 | tf_op jit(solution)/shard_map/ppermute | solution.py:215
  221.0 1.5 copy-start
Sparse Core Ops, SparseCore 0:
  11.2 107.2 all-gather.2
  121.6 85.9 all-gather.4
  231.5 80.4 all-reduce.5

commit v2 on v1

--- a/solution.py
+++ b/solution.py
@@ -150,13 +150,14 @@
         acc[...] = jnp.zeros_like(acc)
 
     source = lax.broadcasted_iota(jnp.int32, (rows, rows), 0)
-    side = side_ref[0]
+    side, twin_bit = side_ref[0], side_ref[1]
     pieces = []
     acts = []
     for pair in range(pairs):
         for act_ref, core in ((mine_ref, side), (other_ref, 1 - side)):
-            near = near_ref[pair, core]
-            cot = cot_ref[pair, core]
+            bit = twin_bit if pair == 0 else 1 - twin_bit
+            near = near_ref[0, bit, core]
+            cot = cot_ref[0, bit, core]
             parts = []
             for tap in range(taps):
                 other_tap = taps - 1 - tap
@@ -170,33 +171,37 @@
 
     @pl.when(step == pl.num_programs(0) - 1)
     def _():
-        out_ref[:, taps * channels :] = time_ref[...]
-        for tap in range(taps):
-            out_ref[:, tap * channels : (tap + 1) * channels] = (
-                acc[tap * owned : (tap + 1) * owned, :] * scale
-            )
-
-
-def weight_grad(side, near, cot, mine, other, time_part, taps, owned, scale):
+        wide = jnp.concatenate(
+            [acc[tap * owned : (tap + 1) * owned, :] * scale for tap in range(taps)]
+            + [time_ref[...]],
+            axis=1,
+        )
+        share = out_ref.shape[2]
+        for index in range(out_ref.shape[0]):
+            out_ref[index] = wide[:, index * share : (index + 1) * share]
+
+
+def weight_grad(side, near, cot, mine, other, time_part, taps, owned, scale, replicas):
     half, rows, channels = mine.shape
     pairs = 2
-    deep = cot.shape[2]
+    share = (taps * channels + TIME_WIDTH) // replicas
+    deep = cot.shape[3]
     return pl.pallas_call(
         functools.partial(weight_kernel, taps, owned, scale),
         grid_spec=pltpu.PrefetchScalarGridSpec(
             num_scalar_prefetch=1,
             grid=(half // pairs,),
             in_specs=[
-                pl.BlockSpec((pairs, 2, TAP_ROWS, rows), lambda g, s: (g, 0, 0, 0)),
-                pl.BlockSpec((pairs, 2, deep, rows), lambda g, s: (g, 0, 0, 0)),
+                pl.BlockSpec((1, 2, 2, TAP_ROWS, rows), lambda g, s: (s[2 + g], 0, 0, 0, 0)),
+                pl.BlockSpec((1, 2, 2, deep, rows), lambda g, s: (s[2 + g], 0, 0, 0, 0)),
                 pl.BlockSpec((pairs, rows, channels), lambda g, s: (g, 0, 0)),
                 pl.BlockSpec((pairs, rows, channels), lambda g, s: (g, 0, 0)),
                 pl.BlockSpec((owned, TIME_WIDTH), lambda g, s: (0, 0)),
             ],
-            out_specs=pl.BlockSpec((owned, taps * channels + TIME_WIDTH), lambda g, s: (0, 0)),
+            out_specs=pl.BlockSpec((replicas, owned, share), lambda g, s: (0, 0, 0)),
             scratch_shapes=[pltpu.VMEM((taps * owned, channels), jnp.float32)],
         ),
-        out_shape=jax.ShapeDtypeStruct((owned, taps * channels + TIME_WIDTH), jnp.float32),
+        out_shape=jax.ShapeDtypeStruct((replicas, owned, share), jnp.float32),
         cost_estimate=pl.CostEstimate(
             flops=4 * half * rows * channels * taps * owned,
             bytes_accessed=4 * half * rows * channels,
@@ -206,9 +211,52 @@
     )(side, near, cot, mine, other, time_part)
 
 
-def gather_half(block, holders):
-    groups = [list(range(core, holders, 2)) for core in (0, 1)]
-    return lax.all_gather(block, "fsdp", axis=0, tiled=True, axis_index_groups=groups)
+def ring_offsets(length):
+    offsets = [0]
+    for hop in range(1, length // 2 + 1):
+        offsets.append(hop)
+        if hop != length - hop:
+            offsets.append(length - hop)
+    return offsets
+
+
+def ring_gathers(early, late, beside, holders):
+    length = holders // 4
+    twins = [(i, i ^ 2) for i in range(holders)]
+    move = lambda step: [(i, (i // 4 + step) % length * 4 + i % 4) for i in range(holders)]
+    send = lambda block, perm: lax.ppermute(block, "fsdp", perm)
+    hops = length // 2
+    pieces = [{}, {}]
+    flows = [None, None]
+    early_twin = send(early, twins)
+    flows[0] = [jnp.stack([early, early_twin])] * 2
+    pieces[0][0] = flows[0][0]
+    for stage in range(1, hops + 2):
+        if stage == 1:
+            (pair0, late) = lax.optimization_barrier((flows[0][0], late))
+            flows[0] = [pair0, pair0]
+            pieces[0][0] = pair0
+        else:
+            if stage == hops:
+                flows, beside = lax.optimization_barrier((flows, beside))
+            else:
+                flows = lax.optimization_barrier(flows)
+            flows = list(flows)
+        for which in (0, 1):
+            hop = stage - which
+            if hop == 0:
+                flows[1] = [jnp.stack([late, send(late, twins)])] * 2
+                pieces[1][0] = flows[1][0]
+            elif hop <= hops:
+                ahead, behind = flows[which]
+                ahead = send(ahead, move(-1))
+                pieces[which][hop] = ahead
+                if hop != length - hop:
+                    behind = send(behind, move(1))
+                    pieces[which][length - hop] = behind
+                flows[which] = [ahead, behind]
+    order = ring_offsets(length)
+    return [jnp.concatenate([each[place] for place in order], axis=0) for each in pieces] + [beside]
 
 
 def from_partner(block, holders):
@@ -227,13 +275,15 @@
     holders = lax.axis_size("fsdp")
     scale = 1.0 / math.sqrt(replicas * holders * rows)
     feature_count = time_weight.shape[1]
-    side = lax.axis_index("fsdp") % 2
+    holder = lax.axis_index("fsdp")
+    side, twin_bit, place = holder % 2, holder // 2 % 2, holder // 4
+    length = holders // 4
+    offsets = ring_offsets(length)
 
     both = jnp.concatenate(
         [conv_weight, time_weight, jnp.zeros((owned, TIME_WIDTH - feature_count), jnp.bfloat16)],
         axis=1,
     )
-    mine = gather_half(both, holders)
 
     near_all, live_all, member_all = layout(heights, widths, rows)
     near, live, member = near_all[0], live_all[0], member_all[0].T
@@ -259,7 +309,6 @@
     shifted = normed * norm_gain[None, :] + norm_shift[None, :]
     sigmoid_value = jax.nn.sigmoid(shifted)
     activated = (shifted * sigmoid_value).astype(jnp.bfloat16)
-    act_mine = gather_half(activated, holders)
 
     told = swapped[:, owned, : 4 * images].astype(jnp.int32)
     group_near, _, group_member = layout(told[:, :images], told[:, images : 2 * images], rows)
@@ -269,24 +318,39 @@
         "bmr,bor->bmo", group_member, swapped[:, :owned].astype(jnp.float32), precision=highest
     ).reshape(holders * images, owned)
     time_part = jnp.dot(per_image.T, group_embed.astype(jnp.float32), precision=highest) * scale
-    near_flat = group_near.reshape(holders // 2, 2, TAP_ROWS, rows)
-    mine, near_flat, time_part = lax.optimization_barrier((mine, near_flat, time_part))
+    near_flat = group_near.reshape(length, 2, 2, TAP_ROWS, rows)
+    mine, act_mine, (near_flat, time_part) = ring_gathers(
+        both, activated, (near_flat, time_part), holders
+    )
+    mine = mine.reshape(holders // 2 * owned, -1)
     other = from_partner(mine, holders)
 
     embed = timestep_features(timesteps[0], feature_count)
     embed_rows = jnp.dot(member, embed.astype(jnp.float32), precision=highest).astype(jnp.bfloat16)
     embed_rows = jnp.pad(embed_rows, ((0, 0), (0, TIME_WIDTH - feature_count)))
     natural = jnp.arange(outs, dtype=jnp.int32)
-    slot = (natural // (2 * owned)) * owned + natural % owned
-    slot = slot + jnp.where((natural // owned) % 2 == side, 0, outs // 2)
+    owner = natural // owned
+    away = (owner // 4 - place) % length
+    spot = jnp.zeros_like(natural)
+    for index, offset in enumerate(offsets):
+        spot = jnp.where(away == offset, index, spot)
+    slot = (spot * 2 + jnp.where(owner // 2 % 2 == twin_bit, 0, 1)) * owned + natural % owned
+    slot = slot + jnp.where(owner % 2 == side, 0, outs // 2)
     order = (slot[:, None] == natural[None, :]).astype(jnp.bfloat16)
     block_out, grad_act = conv_both(activated, cotan_live, near, order, embed_rows, mine, other, taps)
-    act_mine, grad_act = lax.optimization_barrier((act_mine, grad_act))
     act_other = from_partner(act_mine, holders)
 
     grad_shifted = grad_act * sigmoid_value * (1.0 + shifted * (1.0 - sigmoid_value))
     gain_term = jnp.sum(grad_shifted * normed, axis=0) * scale
     shift_term = jnp.sum(grad_shifted, axis=0) * scale
+    terms = jnp.stack([gain_term, shift_term])
+    terms = jnp.pad(terms, ((0, 6), (0, (taps * channels + TIME_WIDTH) // replicas - channels)))
+    gain_rows = jnp.sum(
+        lax.all_to_all(
+            jnp.broadcast_to(terms[None], (holders,) + terms.shape), "fsdp", 0, 0, tiled=True
+        ),
+        axis=0,
+    )
     grad_normed = grad_shifted * norm_gain[None, :]
     mean_grad = group_mean(grad_normed, member, counts)
     mean_cross = group_mean(grad_normed * normed, member, counts)
@@ -295,21 +359,28 @@
     )
 
     parts = weight_grad(
-        side.astype(jnp.int32)[None],
+        jnp.stack([side, twin_bit] + [(place + offset) % length for offset in offsets]).astype(
+            jnp.int32
+        ),
         near_flat,
-        swapped.reshape(holders // 2, 2, owned + EXTRA, rows),
-        act_mine.reshape(holders // 2, rows, channels),
-        act_other.reshape(holders // 2, rows, channels),
+        swapped.reshape(length, 2, 2, owned + EXTRA, rows),
+        act_mine,
+        act_other,
         jnp.pad(time_part, ((0, 0), (0, TIME_WIDTH - feature_count))),
         taps,
         owned,
         scale,
-    )
-    parts, gain_term, shift_term = lax.optimization_barrier((parts, gain_term, shift_term))
-    joined = lax.psum(parts, "dp")
-    grad_gain, grad_shift = lax.psum((gain_term, shift_term), ("dp", "fsdp"))
+        replicas,
+    )
+    share = parts.shape[2]
+    summed = jnp.sum(lax.all_to_all(parts, "dp", 0, 0, tiled=True), axis=0)
+    own = jnp.concatenate([summed, gain_rows], axis=0)
+    spread = lax.all_to_all(jnp.broadcast_to(own[None], (replicas,) + own.shape), "dp", 0, 0, tiled=True)
+    joined = jnp.transpose(spread[:, :owned], (1, 0, 2)).reshape(owned, replicas * share)
     grad_conv = joined[:, : taps * channels]
     grad_time = joined[:, taps * channels : taps * channels + feature_count]
+    gains = jnp.sum(spread[:, owned:], axis=0)[:2, :channels]
+    grad_gain, grad_shift = gains[0], gains[1]
     return (block_out, grad_features, grad_conv, grad_time, grad_gain, grad_shift)
 
 

time: 324 us -> 222 us (0.69)
  blocking collectives: 76.8 us -> 0 us
  waiting for transfers between devices: 144 us -> 97.1 us
  starting transfers between devices: 11.7 us -> 48.6 us
  between operations: 16.7 us -> 4 us
  matrix products: 9.96 us -> 6.33 us
    all_gather x2 -> x0, waiting for transfers between devices: 137 us -> none  [gather_half(): lax.all_gather(block, 'fsdp', axis=0, tiled=True, axis_index_groups=groups)]
    psum x1 -> x0, blocking collectives: 76.8 us -> none  [shards(): grad_gain, grad_shift = lax.psum((gain_term, shift_term), ('dp', 'fsdp'))]
    ppermute x0 -> x16, waiting for transfers between devices: none -> 65 us  [ring_gathers(): send = lambda block, perm: lax.ppermute(block, 'fsdp', perm)]
    all_to_all x0 -> x3, waiting for transfers between devices: none -> 32.2 us  [the longest x1 21.3 us: shards(): lax.all_to_all(jnp.broadcast_to(terms[None], (holders,) + terms.shape), '...]
    ppermute x0 -> x16, starting transfers between devices: none -> 18.4 us  [ring_gathers(): send = lambda block, perm: lax.ppermute(block, 'fsdp', perm)]
    all_to_all x0 -> x3, starting transfers between devices: none -> 18.4 us  [the longest x1 7.6 us: shards(): lax.all_to_all(jnp.broadcast_to(terms[None], (holders,) + terms.shape), '...]
    dot_general x8, local copies, waits for them, and re-layouts: 7.59 us -> 0.77 us  [group_mean(): sums = jnp.dot(member.T, values, precision=highest)]
    unnamed x18 -> x32, local copies, waits for them, and re-layouts: 1.54 us -> 6.45 us
  transfers between devices with their start and end apart: 6 -> 22, of which waited for: 5 -> 12; matrix products, arithmetic and copies ran while one was open for 14% -> 18% of each run, Pallas kernels for 4% -> 10%
where the time goes in v2:
time: 222 us; the launch traced here: 221 us
  waiting for transfers between devices  97.1 us (44%)
  starting transfers between devices  48.6 us (22%)
  local copies, waits for them, and re-layouts  24.2 us (11%)
  Pallas kernels  22.1 us (10%)
  other arithmetic  18.9 us (9%)
  matrix products  6.33 us (3%)
  between operations  4 us (2%)
    ppermute x16, waiting for transfers between devices, ring_gathers(): send = lambda block, perm: lax.ppermute(block, 'fsdp', perm)  65 us
    all_to_all x1, waiting for transfers between devices, shards(): lax.all_to_all(jnp.broadcast_to(terms[None], (holders,) + terms.shape), '...  21.3 us
    ppermute x16, starting transfers between devices, ring_gathers(): send = lambda block, perm: lax.ppermute(block, 'fsdp', perm)  18.4 us
    pallas_call x1, Pallas kernels, conv_both(): pl.pallas_call(functools.partial(conv_kernel, taps), grid=(taps,), in_spe...  12.5 us
    all_to_all x1, starting transfers between devices, shards(): swapped = lax.all_to_all(packed, 'fsdp', 0, 0, tiled=True)  11.7 us
    all_to_all x1, waiting for transfers between devices, shards(): lax.all_to_all(jnp.broadcast_to(own[None], (replicas,) + own.shape), 'dp'...  10.9 us
    pallas_call x1, Pallas kernels, weight_grad(): pl.pallas_call(functools.partial(weight_kernel, taps, owned, scale), grid...  9.61 us
    select_n x6, other arithmetic, layout(): targets.append(jnp.where(valid, first + near_row * width + near_col, rows))  8.1 us
  transfers between devices with their start and end apart: 22, of which 12 were waited for; matrix products, arithmetic and copies ran while one was open for 18% of the time, Pallas kernels for 10%

profile of v2, /device:TPU:4, one launch (start us, length us, event | category | flops | bytes accessed | tf_op | source)
XLA Modules:
  0.0 221.2 jit_solution(3833388441657974058)
XLA Ops:
  8.6 11.7 %all-to-all-start = ((bf16[32,32,128]{2,1,0:T(8,128)(2,1)}), bf16[32,32,128]{2,1,0:T(8,128)(2,1)S(1)}, u32[]{:S(2)}, u32[]{:S(2)}) async-start(bf16[32,32,128]{2,1,0:T(8,128)(2,1)} %pad_maximum_fusion.2), calls=%async_computation | async-start | bytes 524288 | tf_op jit(solution)/shard_map/all_to_all | solution.py:300
  21.7 1.5 fusion.89
  23.2 1.4 fusion.88
  25.5 5.8 %and_select_fusion.12 = (s32[1,1,128]{2,1,0:T(1,128)S(1)}, s32[1,1,128]{2,1,0:T(1,128)S(1)}, pred[1,1,128]{2,1,0:T(4,128)(4,1)S(1)}, s32[1,1,128]{2,1,0:T(1,128)...) fusion(s32[]{:T(128)} %bitcast.3, s32[]{:T(128)} %bitcast.12, ...), kind=kLoop, calls=%fused_computation.203 | loop fusion | flops 6144 | bytes 4144 | tf_op jit(solution)/shard_map/jit(_where)/select_n | solution.py:49
  33.6 1.2 multiply_convert_fusion
  34.8 3.1 %collective-permute-start.1 = (bf16[2,24,6144]{2,1,0:T(8,128)(2,1)S(1)}, bf16[2,24,6144]{2,1,0:T(8,128)(2,1)S(1)}, u32[]{:S(2)}, u32[]{:S(2)}) collective-permute-start(bf16[2,24,6144]{2,1,0:T(8,128)(2,1)S(1)} %pad_maximum_fusion), channel_id=1, source_target_pairs={{0,28},{1,29},{2,30},{3,31},{4,0},{5,1},{6,2},{7,3},{8,4},{9,5},{1... | collective-permute-start | bytes 1769480 | tf_op jit(solution)/shard_map/ppermute | solution.py:227
  38.0 3.0 %collective-permute-start.3 = (bf16[128,640]{1,0:T(8,128)(2,1)S(1)}, bf16[128,640]{1,0:T(8,128)(2,1)S(1)}, u32[]{:S(2)}, u32[]{:S(2)}) collective-permute-start(bf16[128,640]{1,0:T(8,128)(2,1)S(1)} %get-tuple-element.25.act_ref), channel_id=1, source_target_pairs={{0,2},{1,3},{2,0},{3,1},{4,6},{5,7},{6,4},{7,5},{8,10},{9,11},{10,... | collective-permute-start | bytes 491528 | tf_op jit(solution)/shard_map/ppermute | solution.py:227
  41.9 3.3 %collective-permute-done.3 = bf16[128,640]{1,0:T(8,128)(2,1)S(1)} collective-permute-done((bf16[128,640]{1,0:T(8,128)(2,1)S(1)}, bf16[128,640]{1,0:T(8,128)(2,1)S(1)}, u32[]{:S(2)}, u32[]{:S(2)}) %collective-permute-start.3) | collective-permute-done | bytes 163872 | tf_op jit(solution)/shard_map/ppermute | solution.py:227
  48.3 1.8 and_select_fusion
  50.6 1.6 stack.118.near_ref
  54.0 2.0 collective-permute-start.4
  56.1 3.2 %collective-permute-start.6 = (bf16[2,128,640]{2,1,0:T(8,128)(2,1)}, bf16[2,128,640]{2,1,0:T(8,128)(2,1)S(1)}, u32[]{:S(2)}, u32[]{:S(2)}) collective-permute-start(bf16[2,128,640]{2,1,0:T(8,128)(2,1)} %pad_maximum_fusion.1), channel_id=1, source_target_pairs={{0,28},{1,29},{2,30},{3,31},{4,0},{5,1},{6,2},{7,3},{8,4},{9,5},{1... | collective-permute-start | bytes 983048 | tf_op jit(solution)/shard_map/ppermute | solution.py:227
  61.0 14.0 %collective-permute-done.6 = bf16[2,128,640]{2,1,0:T(8,128)(2,1)S(1)} collective-permute-done((bf16[2,128,640]{2,1,0:T(8,128)(2,1)}, bf16[2,128,640]{2,1,0:T(8,128)(2,1)S(1)}, u32[]{:S(2)}, u32[]{:S(2)}) %collective-permute-start.6) | collective-permute-done | bytes 327712 | tf_op jit(solution)/shard_map/ppermute | solution.py:227
  75.0 2.6 %collective-permute-done.7 = bf16[2,128,640]{2,1,0:T(8,128)(2,1)S(1)} collective-permute-done((bf16[2,128,640]{2,1,0:T(8,128)(2,1)}, bf16[2,128,640]{2,1,0:T(8,128)(2,1)S(1)}, u32[]{:S(2)}, u32[]{:S(2)}) %collective-permute-start.7) | collective-permute-done | bytes 327712 | tf_op jit(solution)/shard_map/ppermute | solution.py:227
  77.9 1.7 collective-permute-start.9
  79.6 1.6 collective-permute-start.10
  83.4 13.7 %collective-permute-done.10 = bf16[2,128,640]{2,1,0:T(8,128)(2,1)S(1)} collective-permute-done((bf16[2,128,640]{2,1,0:T(8,128)(2,1)S(1)}, bf16[2,128,640]{2,1,0:T(8,128)(2,1)S(1)}, u32[]{:S(2)}, u32[]{:S(2)}) %collective-permute-start.10) | collective-permute-done | bytes 327712 | tf_op jit(solution)/shard_map/ppermute | solution.py:227
  97.0 1.6 collective-permute-done.11
  100.7 9.4 %collective-permute-done.12 = bf16[2,24,6144]{2,1,0:T(8,128)(2,1)S(1)} collective-permute-done((bf16[2,24,6144]{2,1,0:T(8,128)(2,1)S(1)}, bf16[2,24,6144]{2,1,0:T(8,128)(2,1)S(1)}, u32[]{:S(2)}, u32[]{:S(2)}) %collective-permute-start.12) | collective-permute-done | bytes 589856 | tf_op jit(solution)/shard_map/ppermute | solution.py:227
  111.1 1.9 collective-permute-start.14
  113.3 8.0 %collective-permute-done.14 = bf16[2,128,640]{2,1,0:T(8,128)(2,1)S(1)} collective-permute-done((bf16[2,128,640]{2,1,0:T(8,128)(2,1)S(1)}, bf16[2,128,640]{2,1,0:T(8,128)(2,1)S(1)}, u32[]{:S(2)}, u32[]{:S(2)}) %collective-permute-start.14) | collective-permute-done | bytes 327712 | tf_op jit(solution)/shard_map/ppermute | solution.py:227
  121.3 2.8 %collective-permute-done.15 = bf16[2,128,640]{2,1,0:T(8,128)(2,1)S(1)} collective-permute-done((bf16[2,128,640]{2,1,0:T(8,128)(2,1)S(1)}, bf16[2,128,640]{2,1,0:T(8,128)(2,1)S(1)}, u32[]{:S(2)}, u32[]{:S(2)}) %collective-permute-start.15) | collective-permute-done | bytes 327712 | tf_op jit(solution)/shard_map/ppermute | solution.py:227
  124.5 8.6 %collective-permute-done.16 = bf16[2,128,640]{2,1,0:T(8,128)(2,1)S(1)} collective-permute-done((bf16[2,128,640]{2,1,0:T(8,128)(2,1)S(1)}, bf16[2,128,640]{2,1,0:T(8,128)(2,1)S(1)}, u32[]{:S(2)}, u32[]{:S(2)}) %collective-permute-start.16) | collective-permute-done | bytes 327712 | tf_op jit(solution)/shard_map/ppermute | solution.py:227
  135.4 1.2 stack.109
  137.4 1.3 fusion.order_ref
  139.3 9.6 %weight_grad.1 = f32[8,24,768]{2,1,0:T(8,128)} custom-call(s32[10]{0:T(128)} %stack.130.side_ref, s32[8,2,2,16,128]{4,3,2,1,0:T(8,128)} %stack.118.near_ref, bf16[8,2,2,32,128]{4,3,2,1,0:T(8,128)(2,1)} %bitcast.87, bf16[16,128,640]{2,1,0:T(8,128)(2,1)} %copy-done, bf16[16,128,640]{2,1,0:T(8,128)(2,1)} %collective-permute-done.17.other_ref, ...), custom_call_target="tpu_custom_call" | custom-call | flops 1132462080 | bytes 5242880 | tf_op jit(solution)/shard_map/weight_grad/pallas_call | solution.py:189
  148.9 5.1 %all-to-all-start.1 = ((f32[8,24,768]{2,1,0:T(8,128)}), f32[8,24,768]{2,1,0:T(8,128)S(1)}, u32[]{:S(2)}, u32[]{:S(2)}) async-start(f32[8,24,768]{2,1,0:T(8,128)} %weight_grad.1), calls=%async_computation.1 | async-start | bytes 1179648 | tf_op jit(solution)/shard_map/all_to_all | solution.py:376
  154.0 12.5 %conv_both.1 = (bf16[128,768]{1,0:T(8,128)(2,1)}, f32[128,640]{1,0:T(8,128)}) custom-call(bf16[128,640]{1,0:T(8,128)(2,1)} %copy-done.1, bf16[128,768]{1,0:T(8,128)(2,1)} %broadcast_select_fusion.cot_ref, s32[16,128]{1,0:T(8,128)} %bitcast.93, bf16[768,768]{1,0:T(8,128)(2,1)} %fusion.order_ref, bf16[128,384]{1,0:T(8,128)(2,1)} %pad.16.embed_ref, ...), custom_call_target="tpu_custom_call" | custom-call | flops 2264924160 | bytes 8847360 | tf_op jit(solution)/shard_map/conv_both/pallas_call | solution.py:111
  168.6 7.6 %all-to-all-start.2 = ((f32[32,8,768]{2,1,0:T(8,128)}), f32[32,8,768]{2,1,0:T(8,128)S(1)}, u32[]{:S(2)}, u32[]{:S(2)}) async-start(f32[32,8,768]{2,1,0:T(8,128)} %broadcast_in_dim.311), calls=%async_computation.2 | async-start | bytes 1572864 | tf_op jit(solution)/shard_map/all_to_all | solution.py:349
  178.3 21.3 %all-to-all-done.2 = f32[32,8,768]{2,1,0:T(8,128)S(1)} async-done(((f32[32,8,768]{2,1,0:T(8,128)}), f32[32,8,768]{2,1,0:T(8,128)S(1)}, u32[]{:S(2)}, u32[]{:S(2)}) %all-to-all-start.2) | async-done | bytes 786464 | tf_op jit(solution)/shard_map/all_to_all | solution.py:349
  200.6 5.7 %all-to-all-start.3 = ((f32[8,32,768]{2,1,0:T(8,128)}), f32[8,32,768]{2,1,0:T(8,128)S(1)}, u32[]{:S(2)}, u32[]{:S(2)}) async-start(f32[8,32,768]{2,1,0:T(8,128)} %broadcast_in_dim.312), calls=%async_computation.3 | async-start | bytes 1572864 | tf_op jit(solution)/shard_map/all_to_all | solution.py:378
  208.2 10.9 %all-to-all-done.3 = f32[8,32,768]{2,1,0:T(8,128)S(1)} async-done(((f32[8,32,768]{2,1,0:T(8,128)}), f32[8,32,768]{2,1,0:T(8,128)S(1)}, u32[]{:S(2)}, u32[]{:S(2)}) %all-to-all-start.3) | async-done | bytes 786464 | tf_op jit(solution)/shard_map/all_to_all | solution.py:378
  (157 shorter events, 36.8 us)
Async XLA Ops:
  0.6 24.6 %copy-start.4 = (bf16[128,640]{1,0:T(8,128)(2,1)S(1)}, bf16[128,640]{1,0:T(8,128)(2,1)}, u32[]{:S(2)}) copy-start(bf16[128,640]{1,0:T(8,128)(2,1)} %param.9) | copy-start | bytes 491524
  8.6 25.0 %copy-start.6 = (f32[640]{0:T(1024)S(1)}, f32[640]{0:T(1024)}, u32[]{:S(2)}) copy-start(f32[640]{0:T(1024)} %param.13) | copy-start | bytes 7684
  8.6 25.0 %copy-start.7 = (f32[640]{0:T(1024)S(1)}, f32[640]{0:T(1024)}, u32[]{:S(2)}) copy-start(f32[640]{0:T(1024)} %param.14) | copy-start | bytes 7684
  8.6 37.3 %all-to-all-start = ((bf16[32,32,128]{2,1,0:T(8,128)(2,1)}), bf16[32,32,128]{2,1,0:T(8,128)(2,1)S(1)}, u32[]{:S(2)}, u32[]{:S(2)}) async-start(bf16[32,32,128]{2,1,0:T(8,128)(2,1)} %pad_maximum_fusion.2), calls=%async_computation | async-start | bytes 524288 | tf_op jit(solution)/shard_map/all_to_all | solution.py:300
  21.4 13.4 %collective-permute-start = (bf16[24,6144]{1,0:T(8,128)(2,1)S(1)}, bf16[24,6144]{1,0:T(8,128)(2,1)S(1)}, u32[]{:S(2)}, u32[]{:S(2)}) collective-permute-start(bf16[24,6144]{1,0:T(8,128)(2,1)S(1)} %concatenate.37), channel_id=1, source_target_pairs={{0,2},{1,3},{2,0},{3,1},{4,6},{5,7},{6,4},{7,5},{8,10},{9,11},{10,... | collective-permute-start | bytes 884744 | tf_op jit(solution)/shard_map/ppermute | solution.py:227
  34.8 76.3 %copy-start.1 = (bf16[128,640]{1,0:T(8,128)(2,1)}, bf16[128,640]{1,0:T(8,128)(2,1)S(1)}, u32[]{:S(2)}) copy-start(bf16[128,640]{1,0:T(8,128)(2,1)S(1)} %get-tuple-element.25.act_ref) | copy-start | bytes 491524
  34.8 18.1 %collective-permute-start.1 = (bf16[2,24,6144]{2,1,0:T(8,128)(2,1)S(1)}, bf16[2,24,6144]{2,1,0:T(8,128)(2,1)S(1)}, u32[]{:S(2)}, u32[]{:S(2)}) collective-permute-start(bf16[2,24,6144]{2,1,0:T(8,128)(2,1)S(1)} %pad_maximum_fusion), channel_id=1, source_target_pairs={{0,28},{1,29},{2,30},{3,31},{4,0},{5,1},{6,2},{7,3},{8,4},{9,5},{1... | collective-permute-start | bytes 1769480 | tf_op jit(solution)/shard_map/ppermute | solution.py:227
  38.0 16.0 %collective-permute-start.2 = (bf16[2,24,6144]{2,1,0:T(8,128)(2,1)S(1)}, bf16[2,24,6144]{2,1,0:T(8,128)(2,1)S(1)}, u32[]{:S(2)}, u32[]{:S(2)}) collective-permute-start(bf16[2,24,6144]{2,1,0:T(8,128)(2,1)S(1)} %pad_maximum_fusion), channel_id=1, source_target_pairs={{0,4},{1,5},{2,6},{3,7},{4,8},{5,9},{6,10},{7,11},{8,12},{9,13},{1... | collective-permute-start | bytes 1769480 | tf_op jit(solution)/shard_map/ppermute | solution.py:227
  38.0 7.2 %collective-permute-start.3 = (bf16[128,640]{1,0:T(8,128)(2,1)S(1)}, bf16[128,640]{1,0:T(8,128)(2,1)S(1)}, u32[]{:S(2)}, u32[]{:S(2)}) collective-permute-start(bf16[128,640]{1,0:T(8,128)(2,1)S(1)} %get-tuple-element.25.act_ref), channel_id=1, source_target_pairs={{0,2},{1,3},{2,0},{3,1},{4,6},{5,7},{6,4},{7,5},{8,10},{9,11},{10,... | collective-permute-start | bytes 491528 | tf_op jit(solution)/shard_map/ppermute | solution.py:227
  46.0 36.5 %copy-start.2 = (bf16[32,32,128]{2,1,0:T(8,128)(2,1)}, bf16[32,32,128]{2,1,0:T(8,128)(2,1)S(1)}, u32[]{:S(2)}) copy-start(bf16[32,32,128]{2,1,0:T(8,128)(2,1)S(1)} %all-to-all-done) | copy-start | bytes 786436
  54.0 23.5 %collective-permute-start.4 = (bf16[2,24,6144]{2,1,0:T(8,128)(2,1)S(1)}, bf16[2,24,6144]{2,1,0:T(8,128)(2,1)S(1)}, u32[]{:S(2)}, u32[]{:S(2)}) collective-permute-start(bf16[2,24,6144]{2,1,0:T(8,128)(2,1)S(1)} %collective-permute-done.1), channel_id=1, source_target_pairs={{0,28},{1,29},{2,30},{3,31},{4,0},{5,1},{6,2},{7,3},{8,4},{9,5},{1... | collective-permute-start | bytes 1769480 | tf_op jit(solution)/shard_map/ppermute | solution.py:227
  56.0 21.6 %collective-permute-start.5 = (bf16[2,24,6144]{2,1,0:T(8,128)(2,1)S(1)}, bf16[2,24,6144]{2,1,0:T(8,128)(2,1)S(1)}, u32[]{:S(2)}, u32[]{:S(2)}) collective-permute-start(bf16[2,24,6144]{2,1,0:T(8,128)(2,1)S(1)} %collective-permute-done.2), channel_id=1, source_target_pairs={{0,4},{1,5},{2,6},{3,7},{4,8},{5,9},{6,10},{7,11},{8,12},{9,13},{1... | collective-permute-start | bytes 1769480 | tf_op jit(solution)/shard_map/ppermute | solution.py:227
  56.1 18.9 %collective-permute-start.6 = (bf16[2,128,640]{2,1,0:T(8,128)(2,1)}, bf16[2,128,640]{2,1,0:T(8,128)(2,1)S(1)}, u32[]{:S(2)}, u32[]{:S(2)}) collective-permute-start(bf16[2,128,640]{2,1,0:T(8,128)(2,1)} %pad_maximum_fusion.1), channel_id=1, source_target_pairs={{0,28},{1,29},{2,30},{3,31},{4,0},{5,1},{6,2},{7,3},{8,4},{9,5},{1... | collective-permute-start | bytes 983048 | tf_op jit(solution)/shard_map/ppermute | solution.py:227
  59.2 18.3 %collective-permute-start.7 = (bf16[2,128,640]{2,1,0:T(8,128)(2,1)}, bf16[2,128,640]{2,1,0:T(8,128)(2,1)S(1)}, u32[]{:S(2)}, u32[]{:S(2)}) collective-permute-start(bf16[2,128,640]{2,1,0:T(8,128)(2,1)} %pad_maximum_fusion.1), channel_id=1, source_target_pairs={{0,4},{1,5},{2,6},{3,7},{4,8},{5,9},{6,10},{7,11},{8,12},{9,13},{1... | collective-permute-start | bytes 983048 | tf_op jit(solution)/shard_map/ppermute | solution.py:227
  77.6 21.0 %collective-permute-start.8 = (bf16[2,24,6144]{2,1,0:T(8,128)(2,1)S(1)}, bf16[2,24,6144]{2,1,0:T(8,128)(2,1)S(1)}, u32[]{:S(2)}, u32[]{:S(2)}) collective-permute-start(bf16[2,24,6144]{2,1,0:T(8,128)(2,1)S(1)} %collective-permute-done.4), channel_id=1, source_target_pairs={{0,28},{1,29},{2,30},{3,31},{4,0},{5,1},{6,2},{7,3},{8,4},{9,5},{1... | collective-permute-start | bytes 1769480 | tf_op jit(solution)/shard_map/ppermute | solution.py:227
  77.9 20.7 %collective-permute-start.9 = (bf16[2,24,6144]{2,1,0:T(8,128)(2,1)S(1)}, bf16[2,24,6144]{2,1,0:T(8,128)(2,1)S(1)}, u32[]{:S(2)}, u32[]{:S(2)}) collective-permute-start(bf16[2,24,6144]{2,1,0:T(8,128)(2,1)S(1)} %collective-permute-done.5), channel_id=1, source_target_pairs={{0,4},{1,5},{2,6},{3,7},{4,8},{5,9},{6,10},{7,11},{8,12},{9,13},{1... | collective-permute-start | bytes 1769480 | tf_op jit(solution)/shard_map/ppermute | solution.py:227
  79.6 17.4 %collective-permute-start.10 = (bf16[2,128,640]{2,1,0:T(8,128)(2,1)S(1)}, bf16[2,128,640]{2,1,0:T(8,128)(2,1)S(1)}, u32[]{:S(2)}, u32[]{:S(2)}) collective-permute-start(bf16[2,128,640]{2,1,0:T(8,128)(2,1)S(1)} %collective-permute-done.6), channel_id=1, source_target_pairs={{0,28},{1,29},{2,30},{3,31},{4,0},{5,1},{6,2},{7,3},{8,4},{9,5},{1... | collective-permute-start | bytes 983048 | tf_op jit(solution)/shard_map/ppermute | solution.py:227
  81.2 17.4 %collective-permute-start.11 = (bf16[2,128,640]{2,1,0:T(8,128)(2,1)S(1)}, bf16[2,128,640]{2,1,0:T(8,128)(2,1)S(1)}, u32[]{:S(2)}, u32[]{:S(2)}) collective-permute-start(bf16[2,128,640]{2,1,0:T(8,128)(2,1)S(1)} %collective-permute-done.7), channel_id=1, source_target_pairs={{0,4},{1,5},{2,6},{3,7},{4,8},{5,9},{6,10},{7,11},{8,12},{9,13},{1... | collective-permute-start | bytes 983048 | tf_op jit(solution)/shard_map/ppermute | solution.py:227
  98.6 11.5 %collective-permute-start.12 = (bf16[2,24,6144]{2,1,0:T(8,128)(2,1)S(1)}, bf16[2,24,6144]{2,1,0:T(8,128)(2,1)S(1)}, u32[]{:S(2)}, u32[]{:S(2)}) collective-permute-start(bf16[2,24,6144]{2,1,0:T(8,128)(2,1)S(1)} %collective-permute-done.8), channel_id=1, source_target_pairs={{0,28},{1,29},{2,30},{3,31},{4,0},{5,1},{6,2},{7,3},{8,4},{9,5},{1... | collective-permute-start | bytes 1769480 | tf_op jit(solution)/shard_map/ppermute | solution.py:227
  111.0 43.0 %collective-permute-start.13 = (bf16[384,6144]{1,0:T(8,128)(2,1)}, bf16[384,6144]{1,0:T(8,128)(2,1)}, u32[]{:S(2)}, u32[]{:S(2)}) collective-permute-start(bf16[384,6144]{1,0:T(8,128)(2,1)} %bitcast.78), channel_id=1, source_target_pairs={{0,1},{1,0},{2,3},{3,2},{4,5},{5,4},{6,7},{7,6},{8,9},{9,8},{10,11... | collective-permute-start | bytes 14155784 | tf_op jit(solution)/shard_map/ppermute | solution.py:263
  111.1 25.5 %copy-start.3 = (bf16[128,768]{1,0:T(8,128)(2,1)S(1)}, bf16[128,768]{1,0:T(8,128)(2,1)}, u32[]{:S(2)}) copy-start(bf16[128,768]{1,0:T(8,128)(2,1)} %param.17) | copy-start | bytes 589828
  111.1 10.2 %collective-permute-start.14 = (bf16[2,128,640]{2,1,0:T(8,128)(2,1)S(1)}, bf16[2,128,640]{2,1,0:T(8,128)(2,1)S(1)}, u32[]{:S(2)}, u32[]{:S(2)}) collective-permute-start(bf16[2,128,640]{2,1,0:T(8,128)(2,1)S(1)} %collective-permute-done.10), channel_id=1, source_target_pairs={{0,28},{1,29},{2,30},{3,31},{4,0},{5,1},{6,2},{7,3},{8,4},{9,5},{1... | collective-permute-start | bytes 983048 | tf_op jit(solution)/shard_map/ppermute | solution.py:227
  113.0 11.1 %collective-permute-start.15 = (bf16[2,128,640]{2,1,0:T(8,128)(2,1)S(1)}, bf16[2,128,640]{2,1,0:T(8,128)(2,1)S(1)}, u32[]{:S(2)}, u32[]{:S(2)}) collective-permute-start(bf16[2,128,640]{2,1,0:T(8,128)(2,1)S(1)} %collective-permute-done.11), channel_id=1, source_target_pairs={{0,4},{1,5},{2,6},{3,7},{4,8},{5,9},{6,10},{7,11},{8,12},{9,13},{1... | collective-permute-start | bytes 983048 | tf_op jit(solution)/shard_map/ppermute | solution.py:227
  124.1 9.0 %collective-permute-start.16 = (bf16[2,128,640]{2,1,0:T(8,128)(2,1)S(1)}, bf16[2,128,640]{2,1,0:T(8,128)(2,1)S(1)}, u32[]{:S(2)}, u32[]{:S(2)}) collective-permute-start(bf16[2,128,640]{2,1,0:T(8,128)(2,1)S(1)} %collective-permute-done.14), channel_id=1, source_target_pairs={{0,28},{1,29},{2,30},{3,31},{4,0},{5,1},{6,2},{7,3},{8,4},{9,5},{1... | collective-permute-start | bytes 983048 | tf_op jit(solution)/shard_map/ppermute | solution.py:227
  133.2 6.2 %copy-start = (bf16[16,128,640]{2,1,0:T(8,128)(2,1)}, bf16[16,128,640]{2,1,0:T(8,128)(2,1)S(1)}, u32[]{:S(2)}) copy-start(bf16[16,128,640]{2,1,0:T(8,128)(2,1)S(1)} %constant_dynamic-update-slice_fusion.8.mine_ref) | copy-start | bytes 7864324
  133.2 6.1 %collective-permute-start.17 = (bf16[16,128,640]{2,1,0:T(8,128)(2,1)S(1)}, bf16[16,128,640]{2,1,0:T(8,128)(2,1)}, u32[]{:S(2)}, u32[]{:S(2)}) collective-permute-start(bf16[16,128,640]{2,1,0:T(8,128)(2,1)S(1)} %constant_dynamic-update-slice_fusion.8.mine_ref), channel_id=1, source_target_pairs={{0,1},{1,0},{2,3},{3,2},{4,5},{5,4},{6,7},{7,6},{8,9},{9,8},{10,11... | collective-permute-start | bytes 7864328 | tf_op jit(solution)/shard_map/ppermute | solution.py:263
  148.9 18.8 %all-to-all-start.1 = ((f32[8,24,768]{2,1,0:T(8,128)}), f32[8,24,768]{2,1,0:T(8,128)S(1)}, u32[]{:S(2)}, u32[]{:S(2)}) async-start(f32[8,24,768]{2,1,0:T(8,128)} %weight_grad.1), calls=%async_computation.1 | async-start | bytes 1179648 | tf_op jit(solution)/shard_map/all_to_all | solution.py:376
  168.6 30.9 %all-to-all-start.2 = ((f32[32,8,768]{2,1,0:T(8,128)}), f32[32,8,768]{2,1,0:T(8,128)S(1)}, u32[]{:S(2)}, u32[]{:S(2)}) async-start(f32[32,8,768]{2,1,0:T(8,128)} %broadcast_in_dim.311), calls=%async_computation.2 | async-start | bytes 1572864 | tf_op jit(solution)/shard_map/all_to_all | solution.py:349
  176.7 30.4 %copy-start.5 = (f32[128,640]{1,0:T(8,128)S(1)}, f32[128,640]{1,0:T(8,128)}, u32[]{:S(2)}) copy-start(f32[128,640]{1,0:T(8,128)} %get-tuple-element.155) | copy-start | bytes 983044
  200.6 18.5 %all-to-all-start.3 = ((f32[8,32,768]{2,1,0:T(8,128)}), f32[8,32,768]{2,1,0:T(8,128)S(1)}, u32[]{:S(2)}, u32[]{:S(2)}) async-start(f32[8,32,768]{2,1,0:T(8,128)} %broadcast_in_dim.312), calls=%async_computation.3 | async-start | bytes 1572864 | tf_op jit(solution)/shard_map/all_to_all | solution.py:378

commit v3 on v2

--- a/solution.py
+++ b/solution.py
@@ -220,7 +220,7 @@
     return offsets
 
 
-def ring_gathers(early, late, beside, holders):
+def ring_gathers(early, early_twin, late, beside, holders):
     length = holders // 4
     twins = [(i, i ^ 2) for i in range(holders)]
     move = lambda step: [(i, (i // 4 + step) % length * 4 + i % 4) for i in range(holders)]
@@ -228,15 +228,10 @@
     hops = length // 2
     pieces = [{}, {}]
     flows = [None, None]
-    early_twin = send(early, twins)
     flows[0] = [jnp.stack([early, early_twin])] * 2
     pieces[0][0] = flows[0][0]
     for stage in range(1, hops + 2):
-        if stage == 1:
-            (pair0, late) = lax.optimization_barrier((flows[0][0], late))
-            flows[0] = [pair0, pair0]
-            pieces[0][0] = pair0
-        else:
+        if stage > 1:
             if stage == hops:
                 flows, beside = lax.optimization_barrier((flows, beside))
             else:
@@ -249,11 +244,15 @@
                 pieces[1][0] = flows[1][0]
             elif hop <= hops:
                 ahead, behind = flows[which]
-                ahead = send(ahead, move(-1))
-                pieces[which][hop] = ahead
                 if hop != length - hop:
+                    ahead = send(ahead, move(-1))
                     behind = send(behind, move(1))
+                    pieces[which][hop] = ahead
                     pieces[which][length - hop] = behind
+                else:
+                    ahead = send(ahead[:1], move(-1))
+                    behind = send(behind[1:], move(1))
+                    pieces[which][hop] = jnp.concatenate([ahead, behind], axis=0)
                 flows[which] = [ahead, behind]
     order = ring_offsets(length)
     return [jnp.concatenate([each[place] for place in order], axis=0) for each in pieces] + [beside]
@@ -285,6 +284,8 @@
         axis=1,
     )
 
+    twin = lax.ppermute(both, "fsdp", [(i, i ^ 2) for i in range(holders)])
+
     near_all, live_all, member_all = layout(heights, widths, rows)
     near, live, member = near_all[0], live_all[0], member_all[0].T
     cotan_live = jnp.where(live[:, None], cotangent, jnp.zeros_like(cotangent))
@@ -297,6 +298,7 @@
     packed = jnp.concatenate(
         [columns, jnp.broadcast_to(facts[None], (holders, EXTRA, rows))], axis=1
     )
+    packed, features, twin = lax.optimization_barrier((packed, features, twin))
     swapped = lax.all_to_all(packed, "fsdp", 0, 0, tiled=True)
 
     counts = jnp.maximum((heights[0] * widths[0]).astype(jnp.float32) * (channels // GROUPS), 1.0)
@@ -320,7 +322,7 @@
     time_part = jnp.dot(per_image.T, group_embed.astype(jnp.float32), precision=highest) * scale
     near_flat = group_near.reshape(length, 2, 2, TAP_ROWS, rows)
     mine, act_mine, (near_flat, time_part) = ring_gathers(
-        both, activated, (near_flat, time_part), holders
+        both, twin, activated, (near_flat, time_part), holders
     )
     mine = mine.reshape(holders // 2 * owned, -1)
     other = from_partner(mine, holders)
@@ -338,19 +340,24 @@
     slot = slot + jnp.where(owner % 2 == side, 0, outs // 2)
     order = (slot[:, None] == natural[None, :]).astype(jnp.bfloat16)
     block_out, grad_act = conv_both(activated, cotan_live, near, order, embed_rows, mine, other, taps)
-    act_other = from_partner(act_mine, holders)
 
     grad_shifted = grad_act * sigmoid_value * (1.0 + shifted * (1.0 - sigmoid_value))
     gain_term = jnp.sum(grad_shifted * normed, axis=0) * scale
     shift_term = jnp.sum(grad_shifted, axis=0) * scale
-    terms = jnp.stack([gain_term, shift_term])
-    terms = jnp.pad(terms, ((0, 6), (0, (taps * channels + TIME_WIDTH) // replicas - channels)))
+    lanes = 128
+    count = 2 * channels // lanes
+    terms = jnp.stack([gain_term, shift_term]).reshape(count, lanes)
+    terms = jnp.pad(terms, ((0, -count % 8), (0, 0)))
+    act_mine, terms = lax.optimization_barrier((act_mine, terms))
+    act_other = from_partner(act_mine, holders)
     gain_rows = jnp.sum(
         lax.all_to_all(
             jnp.broadcast_to(terms[None], (holders,) + terms.shape), "fsdp", 0, 0, tiled=True
         ),
         axis=0,
-    )
+    )[:count].reshape(2, channels)
+    share = (taps * channels + TIME_WIDTH) // replicas
+    gain_rows = jnp.pad(gain_rows, ((0, 6), (0, share - channels)))
     grad_normed = grad_shifted * norm_gain[None, :]
     mean_grad = group_mean(grad_normed, member, counts)
     mean_cross = group_mean(grad_normed * normed, member, counts)

time: 222 us -> 226 us (1.018)
  waiting for transfers between devices: 97.1 us -> 77.8 us
  local copies, waits for them, and re-layouts: 24.2 us -> 38.4 us
  other arithmetic: 18.9 us -> 24.7 us
    all_to_all x1, waiting for transfers between devices: 21.3 us -> 0.32 us  [shards(): lax.all_to_all(jnp.broadcast_to(terms[None], (holders,) + terms.shape), '...]
    ppermute x16 -> x17, waiting for transfers between devices: 65 us -> 50 us  [ring_gathers(): send = lambda block, perm: lax.ppermute(block, 'fsdp', perm)]
    all_to_all x1, waiting for transfers between devices: 0.01 us -> 8.72 us  [shards(): summed = jnp.sum(lax.all_to_all(parts, 'dp', 0, 0, tiled=True), axis=0)]
    all_to_all x1, waiting for transfers between devices: 0.01 us -> 8.66 us  [shards(): swapped = lax.all_to_all(packed, 'fsdp', 0, 0, tiled=True)]
    unnamed x32 -> x98, local copies, waits for them, and re-layouts: 6.45 us -> 11.9 us
    all_to_all x1, starting transfers between devices: 11.7 us -> 7.75 us  [shards(): swapped = lax.all_to_all(packed, 'fsdp', 0, 0, tiled=True)]
    ppermute x16 -> x17, starting transfers between devices: 18.4 us -> 21.8 us  [ring_gathers(): send = lambda block, perm: lax.ppermute(block, 'fsdp', perm)]
    select_n x6, other arithmetic: 8.1 us -> 10.9 us  [layout(): targets.append(jnp.where(valid, first + near_row * width + near_col, rows))]
  transfers between devices with their start and end apart: 22 -> 24, of which waited for: 12 -> 14; matrix products, arithmetic and copies ran while one was open for 18% -> 28% of each run, Pallas kernels for 10% -> 4%
where the time goes in v3:
time: 226 us; the launch traced here: 225 us
  waiting for transfers between devices  77.8 us (34%)
  starting transfers between devices  49.6 us (22%)
  local copies, waits for them, and re-layouts  38.4 us (17%)
  other arithmetic  24.7 us (11%)
  Pallas kernels  22.9 us (10%)
  matrix products  6.99 us (3%)
  between operations  4.2 us (2%)
    ppermute x17, waiting for transfers between devices, ring_gathers(): send = lambda block, perm: lax.ppermute(block, 'fsdp', perm)  50 us
    ppermute x17, starting transfers between devices, ring_gathers(): send = lambda block, perm: lax.ppermute(block, 'fsdp', perm)  21.8 us
    pallas_call x1, Pallas kernels, conv_both(): pl.pallas_call(functools.partial(conv_kernel, taps), grid=(taps,), in_spe...  13.4 us
    unnamed x98, local copies, waits for them, and re-layouts  11.9 us
    select_n x6, other arithmetic, layout(): targets.append(jnp.where(valid, first + near_row * width + near_col, rows))  10.9 us
    all_to_all x1, waiting for transfers between devices, shards(): lax.all_to_all(jnp.broadcast_to(own[None], (replicas,) + own.shape), 'dp'...  10.1 us
    pallas_call x1, Pallas kernels, weight_grad(): pl.pallas_call(functools.partial(weight_kernel, taps, owned, scale), grid...  9.58 us
    all_to_all x1, starting transfers between devices, shards(): lax.all_to_all(jnp.broadcast_to(terms[None], (holders,) + terms.shape), '...  8.98 us
  transfers between devices with their start and end apart: 24, of which 14 were waited for; matrix products, arithmetic and copies ran while one was open for 28% of the time, Pallas kernels for 4%

profile of v3, /device:TPU:4, one launch (start us, length us, event | category | flops | bytes accessed | tf_op | source)
XLA Modules:
  0.0 224.6 jit_solution(12926099131591833575)
XLA Ops:
  1.7 2.3 %collective-permute-start = (bf16[24,6144]{1,0:T(8,128)(2,1)S(1)}, bf16[24,6144]{1,0:T(8,128)(2,1)S(1)}, u32[]{:S(2)}, u32[]{:S(2)}) collective-permute-start(bf16[24,6144]{1,0:T(8,128)(2,1)S(1)} %concatenate.39), channel_id=1, source_target_pairs={{0,2},{1,3},{2,0},{3,1},{4,6},{5,7},{6,4},{7,5},{8,10},{9,11},{10,... | collective-permute-start | bytes 884744 | tf_op jit(solution)/shard_map/ppermute | solution.py:287
  6.0 1.5 fusion.92
  7.5 1.5 fusion.91
  16.0 6.5 %and_select_fusion.10 = (s32[1,1,128]{2,1,0:T(1,128)}, s32[1,1,128]{2,1,0:T(1,128)}, pred[1,1,128]{2,1,0:T(4,128)(4,1)}, s32[1,1,128]{2,1,0:T(1,128)}, s32[1,1,1...) fusion(s32[]{:T(128)} %bitcast, s32[]{:T(128)} %bitcast.14, ...), kind=kLoop, calls=%fused_computation.205 | loop fusion | flops 6144 | bytes 4144 | tf_op jit(solution)/shard_map/jit(_where)/select_n | solution.py:49
  24.4 4.1 %collective-permute-start.1 = (bf16[2,24,6144]{2,1,0:T(8,128)(2,1)}, bf16[2,24,6144]{2,1,0:T(8,128)(2,1)}, u32[]{:S(2)}, u32[]{:S(2)}) collective-permute-start(bf16[2,24,6144]{2,1,0:T(8,128)(2,1)} %pad_maximum_fusion), channel_id=1, source_target_pairs={{0,28},{1,29},{2,30},{3,31},{4,0},{5,1},{6,2},{7,3},{8,4},{9,5},{1... | collective-permute-start | bytes 1769480 | tf_op jit(solution)/shard_map/ppermute | solution.py:227
  32.3 3.0 %collective-permute-start.3 = (bf16[128,640]{1,0:T(8,128)(2,1)}, bf16[128,640]{1,0:T(8,128)(2,1)S(1)}, u32[]{:S(2)}, u32[]{:S(2)}) collective-permute-start(bf16[128,640]{1,0:T(8,128)(2,1)} %get-tuple-element.70.act_ref), channel_id=1, source_target_pairs={{0,2},{1,3},{2,0},{3,1},{4,6},{5,7},{6,4},{7,5},{8,10},{9,11},{10,... | collective-permute-start | bytes 491528 | tf_op jit(solution)/shard_map/ppermute | solution.py:227
  35.3 7.8 %all-to-all-start = ((bf16[32,32,128]{2,1,0:T(8,128)(2,1)}), bf16[32,32,128]{2,1,0:T(8,128)(2,1)S(1)}, u32[]{:S(2)}, u32[]{:S(2)}) async-start(bf16[32,32,128]{2,1,0:T(8,128)(2,1)} %pad_maximum_fusion.2), calls=%async_computation | async-start | bytes 524288 | tf_op jit(solution)/shard_map/all_to_all | solution.py:302
  43.0 1.7 constant_dynamic-update-slice_fusion.8
  44.7 1.7 pad_maximum_fusion.1
  46.5 8.7 %all-to-all-done = bf16[32,32,128]{2,1,0:T(8,128)(2,1)S(1)} async-done(((bf16[32,32,128]{2,1,0:T(8,128)(2,1)}), bf16[32,32,128]{2,1,0:T(8,128)(2,1)S(1)}, u32[]{:S(2)}, u32[]{:S(2)}) %all-to-all-start) | async-done | bytes 262176 | tf_op jit(solution)/shard_map/all_to_all | solution.py:302
  63.5 2.6 %and_select_fusion = (s32[8,2,2,1,128]{4,3,2,1,0:T(1,128)S(1)}, s32[8,2,2,1,128]{4,3,2,1,0:T(1,128)S(1)}, pred[8,2,2,1,128]{4,3,2,1,0:T(4,128)(4,1)S(1)}, s32[8,...) fusion(s32[8,2,2]{2,1,0:T(2,128)S(1)} %lt.956, ...), kind=kLoop, calls=%fused_computation.57 | loop fusion | flops 196608 | bytes 120320 | tf_op jit(solution)/shard_map/jit(_where)/select_n | solution.py:49
  68.4 3.2 %stack.118.near_ref = s32[8,2,2,16,128]{4,3,2,1,0:T(8,128)} concatenate(s32[8,2,2,1,128]{4,3,2,1,0:T(1,128)} %get-tuple-element.120, s32[8,2,2,1,128]{4,3,2,1,0:T(1,128)} %get-tuple-element.121, s32[8,2,2,1,128]{4,3,2,1,0:T(1,128)} %get-tuple-element.115, s32[8,2,2,1,128]{4,3,2,1,0:T(1,128)} %get-tuple-element.107, s32[8,2,2,1,128]{4,3,2,1,0:T(1,128)} %get-tuple-element.106, ...), dimensions={3} | concatenate | bytes 524288 | tf_op jit(solution)/shard_map/stack | solution.py:51
  73.7 2.0 collective-permute-start.5
  77.7 1.9 constant_dynamic-update-slice_fusion.7
  79.7 1.9 constant_dynamic-update-slice_fusion.6
  81.6 13.9 %collective-permute-done.6 = bf16[2,128,640]{2,1,0:T(8,128)(2,1)S(1)} collective-permute-done((bf16[2,128,640]{2,1,0:T(8,128)(2,1)}, bf16[2,128,640]{2,1,0:T(8,128)(2,1)S(1)}, u32[]{:S(2)}, u32[]{:S(2)}) %collective-permute-start.6) | collective-permute-done | bytes 327712 | tf_op jit(solution)/shard_map/ppermute | solution.py:227
  97.0 1.8 collective-permute-start.9
  102.7 14.8 %collective-permute-done.10 = bf16[2,128,640]{2,1,0:T(8,128)(2,1)S(1)} collective-permute-done((bf16[2,128,640]{2,1,0:T(8,128)(2,1)S(1)}, bf16[2,128,640]{2,1,0:T(8,128)(2,1)S(1)}, u32[]{:S(2)}, u32[]{:S(2)}) %collective-permute-start.10) | collective-permute-done | bytes 327712 | tf_op jit(solution)/shard_map/ppermute | solution.py:227
  119.4 1.8 collective-permute-start.13
  122.9 2.9 %collective-permute-done.12 = bf16[1,24,6144]{2,1,0:T(8,128)(2,1)S(1)} collective-permute-done((bf16[1,24,6144]{2,1,0:T(8,128)(2,1)S(1)}, bf16[1,24,6144]{2,1,0:T(8,128)(2,1)S(1)}, u32[]{:S(2)}, u32[]{:S(2)}) %collective-permute-start.12) | collective-permute-done | bytes 294944 | tf_op jit(solution)/shard_map/ppermute | solution.py:227
  136.2 8.1 %collective-permute-done.15 = bf16[2,128,640]{2,1,0:T(8,128)(2,1)S(1)} collective-permute-done((bf16[2,128,640]{2,1,0:T(8,128)(2,1)}, bf16[2,128,640]{2,1,0:T(8,128)(2,1)S(1)}, u32[]{:S(2)}, u32[]{:S(2)}) %collective-permute-start.15) | collective-permute-done | bytes 327712 | tf_op jit(solution)/shard_map/ppermute | solution.py:227
  144.3 1.7 collective-permute-done.16
  146.8 1.5 collective-permute-start.18
  148.4 3.3 %collective-permute-done.17 = bf16[1,128,640]{2,1,0:T(8,128)(2,1)S(1)} collective-permute-done((bf16[1,128,640]{2,1,0:T(8,128)(2,1)S(1)}, bf16[1,128,640]{2,1,0:T(8,128)(2,1)S(1)}, u32[]{:S(2)}, u32[]{:S(2)}) %collective-permute-start.17) | collective-permute-done | bytes 163872 | tf_op jit(solution)/shard_map/ppermute | solution.py:227
  151.7 1.7 collective-permute-done.18
  153.5 13.4 %conv_both.1 = (bf16[128,768]{1,0:T(8,128)(2,1)}, f32[128,640]{1,0:T(8,128)}) custom-call(bf16[128,640]{1,0:T(8,128)(2,1)} %get-tuple-element.70.act_ref, bf16[128,768]{1,0:T(8,128)(2,1)} %broadcast_select_fusion.cot_ref, s32[16,128]{1,0:T(8,128)} %bitcast.95, bf16[768,768]{1,0:T(8,128)(2,1)} %fusion.order_ref, bf16[128,384]{1,0:T(8,128)(2,1)} %pad.21.embed_ref, ...), custom_call_target="tpu_custom_call" | custom-call | flops 2264924160 | bytes 8847360 | tf_op jit(solution)/shard_map/conv_both/pallas_call | solution.py:111
  168.9 9.0 %all-to-all-start.2 = ((f32[32,16,128]{2,1,0:T(8,128)}), f32[32,16,128]{2,1,0:T(8,128)S(1)}, u32[]{:S(2)}, u32[]{:S(2)}) async-start(f32[32,16,128]{2,1,0:T(8,128)} %broadcast_in_dim.311), calls=%async_computation.2 | async-start | bytes 524288 | tf_op jit(solution)/shard_map/all_to_all | solution.py:354
  180.1 9.6 %weight_grad.1 = f32[8,24,768]{2,1,0:T(8,128)} custom-call(s32[10]{0:T(128)} %stack.130.side_ref, s32[8,2,2,16,128]{4,3,2,1,0:T(8,128)} %stack.118.near_ref, bf16[8,2,2,32,128]{4,3,2,1,0:T(8,128)(2,1)} %bitcast.90, bf16[16,128,640]{2,1,0:T(8,128)(2,1)} %copy-done, bf16[16,128,640]{2,1,0:T(8,128)(2,1)} %collective-permute-done.19.other_ref, ...), custom_call_target="tpu_custom_call" | custom-call | flops 1132462080 | bytes 5242880 | tf_op jit(solution)/shard_map/weight_grad/pallas_call | solution.py:189
  190.0 5.1 %all-to-all-start.1 = ((f32[8,24,768]{2,1,0:T(8,128)}), f32[8,24,768]{2,1,0:T(8,128)S(1)}, u32[]{:S(2)}, u32[]{:S(2)}) async-start(f32[8,24,768]{2,1,0:T(8,128)} %weight_grad.1), calls=%async_computation.1 | async-start | bytes 1179648 | tf_op jit(solution)/shard_map/all_to_all | solution.py:383
  197.2 8.7 %all-to-all-done.1 = f32[8,24,768]{2,1,0:T(8,128)S(1)} async-done(((f32[8,24,768]{2,1,0:T(8,128)}), f32[8,24,768]{2,1,0:T(8,128)S(1)}, u32[]{:S(2)}, u32[]{:S(2)}) %all-to-all-start.1) | async-done | bytes 589856 | tf_op jit(solution)/shard_map/all_to_all | solution.py:383
  206.9 3.5 %all-to-all-start.3 = ((f32[8,32,768]{2,1,0:T(8,128)}), f32[8,32,768]{2,1,0:T(8,128)S(1)}, u32[]{:S(2)}, u32[]{:S(2)}) async-start(f32[8,32,768]{2,1,0:T(8,128)} %broadcast_in_dim.312), calls=%async_computation.3 | async-start | bytes 1572864 | tf_op jit(solution)/shard_map/all_to_all | solution.py:385
  212.3 10.1 %all-to-all-done.3 = f32[8,32,768]{2,1,0:T(8,128)S(1)} async-done(((f32[8,32,768]{2,1,0:T(8,128)}), f32[8,32,768]{2,1,0:T(8,128)S(1)}, u32[]{:S(2)}, u32[]{:S(2)}) %all-to-all-start.3) | async-done | bytes 786464 | tf_op jit(solution)/shard_map/all_to_all | solution.py:385
  (234 shorter events, 59.1 us)
Async XLA Ops:
  0.6 27.9 %copy-start.6 = (bf16[128,640]{1,0:T(8,128)(2,1)S(1)}, bf16[128,640]{1,0:T(8,128)(2,1)}, u32[]{:S(2)}) copy-start(bf16[128,640]{1,0:T(8,128)(2,1)} %param.9) | copy-start | bytes 491524
  1.7 21.7 %collective-permute-start = (bf16[24,6144]{1,0:T(8,128)(2,1)S(1)}, bf16[24,6144]{1,0:T(8,128)(2,1)S(1)}, u32[]{:S(2)}, u32[]{:S(2)}) collective-permute-start(bf16[24,6144]{1,0:T(8,128)(2,1)S(1)} %concatenate.39), channel_id=1, source_target_pairs={{0,2},{1,3},{2,0},{3,1},{4,6},{5,7},{6,4},{7,5},{8,10},{9,11},{10,... | collective-permute-start | bytes 884744 | tf_op jit(solution)/shard_map/ppermute | solution.py:287
  9.0 54.1 %copy-start.29 = (f32[160]{0:T(256)}, f32[160]{0:T(256)S(1)}, u32[]{:S(2)}) copy-start(f32[160]{0:T(256)S(1)} %multiply_exponential_fusion) | copy-start | bytes 1924
  24.4 49.3 %collective-permute-start.1 = (bf16[2,24,6144]{2,1,0:T(8,128)(2,1)}, bf16[2,24,6144]{2,1,0:T(8,128)(2,1)}, u32[]{:S(2)}, u32[]{:S(2)}) collective-permute-start(bf16[2,24,6144]{2,1,0:T(8,128)(2,1)} %pad_maximum_fusion), channel_id=1, source_target_pairs={{0,28},{1,29},{2,30},{3,31},{4,0},{5,1},{6,2},{7,3},{8,4},{9,5},{1... | collective-permute-start | bytes 1769480 | tf_op jit(solution)/shard_map/ppermute | solution.py:227
  28.5 45.2 %collective-permute-start.2 = (bf16[2,24,6144]{2,1,0:T(8,128)(2,1)}, bf16[2,24,6144]{2,1,0:T(8,128)(2,1)}, u32[]{:S(2)}, u32[]{:S(2)}) collective-permute-start(bf16[2,24,6144]{2,1,0:T(8,128)(2,1)} %pad_maximum_fusion), channel_id=1, source_target_pairs={{0,4},{1,5},{2,6},{3,7},{4,8},{5,9},{6,10},{7,11},{8,12},{9,13},{1... | collective-permute-start | bytes 1769480 | tf_op jit(solution)/shard_map/ppermute | solution.py:227
  32.3 12.5 %collective-permute-start.3 = (bf16[128,640]{1,0:T(8,128)(2,1)}, bf16[128,640]{1,0:T(8,128)(2,1)S(1)}, u32[]{:S(2)}, u32[]{:S(2)}) collective-permute-start(bf16[128,640]{1,0:T(8,128)(2,1)} %get-tuple-element.70.act_ref), channel_id=1, source_target_pairs={{0,2},{1,3},{2,0},{3,1},{4,6},{5,7},{6,4},{7,5},{8,10},{9,11},{10,... | collective-permute-start | bytes 491528 | tf_op jit(solution)/shard_map/ppermute | solution.py:227
  35.3 19.8 %all-to-all-start = ((bf16[32,32,128]{2,1,0:T(8,128)(2,1)}), bf16[32,32,128]{2,1,0:T(8,128)(2,1)S(1)}, u32[]{:S(2)}, u32[]{:S(2)}) async-start(bf16[32,32,128]{2,1,0:T(8,128)(2,1)} %pad_maximum_fusion.2), calls=%async_computation | async-start | bytes 524288 | tf_op jit(solution)/shard_map/all_to_all | solution.py:302
  44.7 36.8 %copy-start.4 = (bf16[128,640]{1,0:T(8,128)(2,1)}, bf16[128,640]{1,0:T(8,128)(2,1)S(1)}, u32[]{:S(2)}) copy-start(bf16[128,640]{1,0:T(8,128)(2,1)S(1)} %collective-permute-done.3) | copy-start | bytes 491524
  55.1 46.6 %copy-start.2 = (bf16[32,32,128]{2,1,0:T(8,128)(2,1)}, bf16[32,32,128]{2,1,0:T(8,128)(2,1)S(1)}, u32[]{:S(2)}) copy-start(bf16[32,32,128]{2,1,0:T(8,128)(2,1)S(1)} %all-to-all-done) | copy-start | bytes 786436
  73.7 23.1 %collective-permute-start.4 = (bf16[2,24,6144]{2,1,0:T(8,128)(2,1)}, bf16[2,24,6144]{2,1,0:T(8,128)(2,1)S(1)}, u32[]{:S(2)}, u32[]{:S(2)}) collective-permute-start(bf16[2,24,6144]{2,1,0:T(8,128)(2,1)} %collective-permute-done.1), channel_id=1, source_target_pairs={{0,28},{1,29},{2,30},{3,31},{4,0},{5,1},{6,2},{7,3},{8,4},{9,5},{1... | collective-permute-start | bytes 1769480 | tf_op jit(solution)/shard_map/ppermute | solution.py:227
  73.7 23.1 %collective-permute-start.5 = (bf16[2,24,6144]{2,1,0:T(8,128)(2,1)}, bf16[2,24,6144]{2,1,0:T(8,128)(2,1)S(1)}, u32[]{:S(2)}, u32[]{:S(2)}) collective-permute-start(bf16[2,24,6144]{2,1,0:T(8,128)(2,1)} %collective-permute-done.2), channel_id=1, source_target_pairs={{0,4},{1,5},{2,6},{3,7},{4,8},{5,9},{6,10},{7,11},{8,12},{9,13},{1... | collective-permute-start | bytes 1769480 | tf_op jit(solution)/shard_map/ppermute | solution.py:227
  75.7 19.8 %collective-permute-start.6 = (bf16[2,128,640]{2,1,0:T(8,128)(2,1)}, bf16[2,128,640]{2,1,0:T(8,128)(2,1)S(1)}, u32[]{:S(2)}, u32[]{:S(2)}) collective-permute-start(bf16[2,128,640]{2,1,0:T(8,128)(2,1)} %pad_maximum_fusion.1), channel_id=1, source_target_pairs={{0,28},{1,29},{2,30},{3,31},{4,0},{5,1},{6,2},{7,3},{8,4},{9,5},{1... | collective-permute-start | bytes 983048 | tf_op jit(solution)/shard_map/ppermute | solution.py:227
  77.0 19.8 %collective-permute-start.7 = (bf16[2,128,640]{2,1,0:T(8,128)(2,1)}, bf16[2,128,640]{2,1,0:T(8,128)(2,1)S(1)}, u32[]{:S(2)}, u32[]{:S(2)}) collective-permute-start(bf16[2,128,640]{2,1,0:T(8,128)(2,1)} %pad_maximum_fusion.1), channel_id=1, source_target_pairs={{0,4},{1,5},{2,6},{3,7},{4,8},{5,9},{6,10},{7,11},{8,12},{9,13},{1... | collective-permute-start | bytes 983048 | tf_op jit(solution)/shard_map/ppermute | solution.py:227
  95.4 27.5 %copy-start.9 = (bf16[2,128,640]{2,1,0:T(8,128)(2,1)}, bf16[2,128,640]{2,1,0:T(8,128)(2,1)S(1)}, u32[]{:S(2)}) copy-start(bf16[2,128,640]{2,1,0:T(8,128)(2,1)S(1)} %collective-permute-done.6) | copy-start | bytes 983044
  96.7 22.2 %collective-permute-start.8 = (bf16[2,24,6144]{2,1,0:T(8,128)(2,1)S(1)}, bf16[2,24,6144]{2,1,0:T(8,128)(2,1)S(1)}, u32[]{:S(2)}, u32[]{:S(2)}) collective-permute-start(bf16[2,24,6144]{2,1,0:T(8,128)(2,1)S(1)} %collective-permute-done.4), channel_id=1, source_target_pairs={{0,28},{1,29},{2,30},{3,31},{4,0},{5,1},{6,2},{7,3},{8,4},{9,5},{1... | collective-permute-start | bytes 1769480 | tf_op jit(solution)/shard_map/ppermute | solution.py:227
  97.0 21.9 %collective-permute-start.9 = (bf16[2,24,6144]{2,1,0:T(8,128)(2,1)S(1)}, bf16[2,24,6144]{2,1,0:T(8,128)(2,1)S(1)}, u32[]{:S(2)}, u32[]{:S(2)}) collective-permute-start(bf16[2,24,6144]{2,1,0:T(8,128)(2,1)S(1)} %collective-permute-done.5), channel_id=1, source_target_pairs={{0,4},{1,5},{2,6},{3,7},{4,8},{5,9},{6,10},{7,11},{8,12},{9,13},{1... | collective-permute-start | bytes 1769480 | tf_op jit(solution)/shard_map/ppermute | solution.py:227
  98.8 18.6 %collective-permute-start.10 = (bf16[2,128,640]{2,1,0:T(8,128)(2,1)S(1)}, bf16[2,128,640]{2,1,0:T(8,128)(2,1)S(1)}, u32[]{:S(2)}, u32[]{:S(2)}) collective-permute-start(bf16[2,128,640]{2,1,0:T(8,128)(2,1)S(1)} %collective-permute-done.6), channel_id=1, source_target_pairs={{0,28},{1,29},{2,30},{3,31},{4,0},{5,1},{6,2},{7,3},{8,4},{9,5},{1... | collective-permute-start | bytes 983048 | tf_op jit(solution)/shard_map/ppermute | solution.py:227
  100.3 18.6 %collective-permute-start.11 = (bf16[2,128,640]{2,1,0:T(8,128)(2,1)S(1)}, bf16[2,128,640]{2,1,0:T(8,128)(2,1)S(1)}, u32[]{:S(2)}, u32[]{:S(2)}) collective-permute-start(bf16[2,128,640]{2,1,0:T(8,128)(2,1)S(1)} %collective-permute-done.7), channel_id=1, source_target_pairs={{0,4},{1,5},{2,6},{3,7},{4,8},{5,9},{6,10},{7,11},{8,12},{9,13},{1... | collective-permute-start | bytes 983048 | tf_op jit(solution)/shard_map/ppermute | solution.py:227
  102.7 26.8 %copy-start.33 = (s32[1,1,128]{2,1,0:T(1,128)S(1)}, s32[1,1,128]{2,1,0:T(1,128)}, u32[]{:S(2)}) copy-start(s32[1,1,128]{2,1,0:T(1,128)} %get-tuple-element.85) | copy-start | bytes 1540
  102.7 28.1 %copy-start.3 = (bf16[128,768]{1,0:T(8,128)(2,1)S(1)}, bf16[128,768]{1,0:T(8,128)(2,1)}, u32[]{:S(2)}) copy-start(bf16[128,768]{1,0:T(8,128)(2,1)} %param.17) | copy-start | bytes 589828
  102.7 28.1 %copy-start.32 = (pred[128]{0:T(512)(128)(4,1)S(1)}, pred[128]{0:T(512)(128)(4,1)}, u32[]{:S(2)}) copy-start(pred[128]{0:T(512)(128)(4,1)} %copy-done.31) | copy-start | bytes 388
  119.0 6.8 %collective-permute-start.12 = (bf16[1,24,6144]{2,1,0:T(8,128)(2,1)S(1)}, bf16[1,24,6144]{2,1,0:T(8,128)(2,1)S(1)}, u32[]{:S(2)}, u32[]{:S(2)}) collective-permute-start(bf16[1,24,6144]{2,1,0:T(8,128)(2,1)S(1)} %slice.167), channel_id=1, source_target_pairs={{0,28},{1,29},{2,30},{3,31},{4,0},{5,1},{6,2},{7,3},{8,4},{9,5},{1... | collective-permute-start | bytes 884744 | tf_op jit(solution)/shard_map/ppermute | solution.py:227
  119.4 8.0 %collective-permute-start.13 = (bf16[1,24,6144]{2,1,0:T(8,128)(2,1)S(1)}, bf16[1,24,6144]{2,1,0:T(8,128)(2,1)S(1)}, u32[]{:S(2)}, u32[]{:S(2)}) collective-permute-start(bf16[1,24,6144]{2,1,0:T(8,128)(2,1)S(1)} %slice.168), channel_id=1, source_target_pairs={{0,4},{1,5},{2,6},{3,7},{4,8},{5,9},{6,10},{7,11},{8,12},{9,13},{1... | collective-permute-start | bytes 884744 | tf_op jit(solution)/shard_map/ppermute | solution.py:227
  128.1 25.3 %collective-permute-start.14 = (bf16[384,6144]{1,0:T(8,128)(2,1)}, bf16[384,6144]{1,0:T(8,128)(2,1)}, u32[]{:S(2)}, u32[]{:S(2)}) collective-permute-start(bf16[384,6144]{1,0:T(8,128)(2,1)} %bitcast.81), channel_id=1, source_target_pairs={{0,1},{1,0},{2,3},{3,2},{4,5},{5,4},{6,7},{7,6},{8,9},{9,8},{10,11... | collective-permute-start | bytes 14155784 | tf_op jit(solution)/shard_map/ppermute | solution.py:262
  133.9 10.4 %collective-permute-start.15 = (bf16[2,128,640]{2,1,0:T(8,128)(2,1)}, bf16[2,128,640]{2,1,0:T(8,128)(2,1)S(1)}, u32[]{:S(2)}, u32[]{:S(2)}) collective-permute-start(bf16[2,128,640]{2,1,0:T(8,128)(2,1)} %copy-done.10), channel_id=1, source_target_pairs={{0,28},{1,29},{2,30},{3,31},{4,0},{5,1},{6,2},{7,3},{8,4},{9,5},{1... | collective-permute-start | bytes 983048 | tf_op jit(solution)/shard_map/ppermute | solution.py:227
  134.8 11.3 %collective-permute-start.16 = (bf16[2,128,640]{2,1,0:T(8,128)(2,1)}, bf16[2,128,640]{2,1,0:T(8,128)(2,1)S(1)}, u32[]{:S(2)}, u32[]{:S(2)}) collective-permute-start(bf16[2,128,640]{2,1,0:T(8,128)(2,1)} %copy-done.12), channel_id=1, source_target_pairs={{0,4},{1,5},{2,6},{3,7},{4,8},{5,9},{6,10},{7,11},{8,12},{9,13},{1... | collective-permute-start | bytes 983048 | tf_op jit(solution)/shard_map/ppermute | solution.py:227
  146.1 5.6 %collective-permute-start.17 = (bf16[1,128,640]{2,1,0:T(8,128)(2,1)S(1)}, bf16[1,128,640]{2,1,0:T(8,128)(2,1)S(1)}, u32[]{:S(2)}, u32[]{:S(2)}) collective-permute-start(bf16[1,128,640]{2,1,0:T(8,128)(2,1)S(1)} %slice.169), channel_id=1, source_target_pairs={{0,28},{1,29},{2,30},{3,31},{4,0},{5,1},{6,2},{7,3},{8,4},{9,5},{1... | collective-permute-start | bytes 491528 | tf_op jit(solution)/shard_map/ppermute | solution.py:227
  146.8 6.6 %collective-permute-start.18 = (bf16[1,128,640]{2,1,0:T(8,128)(2,1)S(1)}, bf16[1,128,640]{2,1,0:T(8,128)(2,1)S(1)}, u32[]{:S(2)}, u32[]{:S(2)}) collective-permute-start(bf16[1,128,640]{2,1,0:T(8,128)(2,1)S(1)} %slice.170), channel_id=1, source_target_pairs={{0,4},{1,5},{2,6},{3,7},{4,8},{5,9},{6,10},{7,11},{8,12},{9,13},{1... | collective-permute-start | bytes 491528 | tf_op jit(solution)/shard_map/ppermute | solution.py:227
  168.1 12.0 %collective-permute-start.19 = (bf16[16,128,640]{2,1,0:T(8,128)(2,1)S(1)}, bf16[16,128,640]{2,1,0:T(8,128)(2,1)}, u32[]{:S(2)}, u32[]{:S(2)}) collective-permute-start(bf16[16,128,640]{2,1,0:T(8,128)(2,1)S(1)} %constant_dynamic-update-slice_fusion.10.mine_ref), channel_id=1, source_target_pairs={{0,1},{1,0},{2,3},{3,2},{4,5},{5,4},{6,7},{7,6},{8,9},{9,8},{10,11... | collective-permute-start | bytes 7864328 | tf_op jit(solution)/shard_map/ppermute | solution.py:262
  168.9 21.1 %all-to-all-start.2 = ((f32[32,16,128]{2,1,0:T(8,128)}), f32[32,16,128]{2,1,0:T(8,128)S(1)}, u32[]{:S(2)}, u32[]{:S(2)}) async-start(f32[32,16,128]{2,1,0:T(8,128)} %broadcast_in_dim.311), calls=%async_computation.2 | async-start | bytes 524288 | tf_op jit(solution)/shard_map/all_to_all | solution.py:354
  190.0 15.9 %all-to-all-start.1 = ((f32[8,24,768]{2,1,0:T(8,128)}), f32[8,24,768]{2,1,0:T(8,128)S(1)}, u32[]{:S(2)}, u32[]{:S(2)}) async-start(f32[8,24,768]{2,1,0:T(8,128)} %weight_grad.1), calls=%async_computation.1 | async-start | bytes 1179648 | tf_op jit(solution)/shard_map/all_to_all | solution.py:383
  206.9 15.6 %all-to-all-start.3 = ((f32[8,32,768]{2,1,0:T(8,128)}), f32[8,32,768]{2,1,0:T(8,128)S(1)}, u32[]{:S(2)}, u32[]{:S(2)}) async-start(f32[8,32,768]{2,1,0:T(8,128)} %broadcast_in_dim.312), calls=%async_computation.3 | async-start | bytes 1572864 | tf_op jit(solution)/shard_map/all_to_all | solution.py:385
  (32 other events, 499.5 us)
